TPU v7x, 32 devices: a whole 2x2x4 slice. The times are simulated.
32 devices in a mesh: seq: 16 (over z, y, core), mp: 2 (over x).
Axes of the slice: x: 2, y: 2, z: 4, core: 2. Of those that a mesh axis runs over, the one named last changes fastest.
Arguments:
- shared_qk: bfloat16 [2048, 4096], P('seq', 'mp'), may hold values from -40 to 40
- values: bfloat16 [2048, 4096], P('seq', 'mp'), may hold values from -6 to 6
- buckets: int32 [2048, 32], P('seq', 'mp'), may hold values from 0 to 15, as said below
- counts: int32 [16, 32, 16], P(None, 'mp'), may hold values from 0 to 16, as said below
- w_out: bfloat16 [4096, 4096], P('mp'), may hold values from -0.09375 to 0.09375
Outputs:
- projected: bfloat16 [2048, 4096], P('seq', 'mp')
Inputs may be any that keep to these rules, and one draw needn't show every extreme that they name: `buckets`: in each head at most 16 tokens among rows d * 128 to (d + 1) * 128 - 1 name one bucket, and in each head one bucket is named by exactly 16 tokens of every such group of rows. counts[d, h, b] is the number of rows among d * 128 to (d + 1) * 128 - 1 whose bucket in head h is b.
All inputs are finite; a program needn't handle non-finite values.
Results may differ from a plain program's by a relative error of at most 0.0057.
Values may be sent and summed in bfloat16 or wider, within the bound.
No kernel may reach another device: no remote copies, remote signals or barrier semaphores. Data moves between devices by JAX's collectives and lax.ppermute only.
A program may use at most 64 MiB of HBM per device.

v0:
```python
import functools
import math

import jax
import jax.numpy as jnp
from jax import lax
from jax.experimental import pallas as pl
from jax.experimental.pallas import tpu as pltpu
from jax.sharding import PartitionSpec as P


BLOCK = 256
MASKED = -1e30


SELF_SCORE = -100000.0


def passed_along(shard, axis, by):
    devices = lax.axis_size(axis)
    return lax.ppermute(shard, axis, [(i, (i + by) % devices) for i in range(devices)])


def block_attention(queries, window, window_live):
    head_dim = queries.shape[-1]
    block_rows = queries.shape[-2]
    key_rows = window[..., :head_dim]
    value_rows = window[..., head_dim:]
    scores = jnp.einsum("cqd,ckd->cqk", queries, key_rows, preferred_element_type=jnp.float32) * (
        1.0 / math.sqrt(head_dim)
    )
    query_place = jnp.arange(block_rows)[:, None] + block_rows
    key_place = jnp.arange(2 * block_rows)[None, :]
    itself = query_place == key_place
    scores = jnp.where(itself[None], SELF_SCORE, scores)
    allowed = window_live[:, None, :] | itself[None]
    row_max = jnp.max(jnp.where(allowed, scores, -1e30), axis=-1, keepdims=True)
    exp_terms = jnp.where(allowed, jnp.exp(scores - row_max), 0.0)
    weights = (exp_terms / jnp.sum(exp_terms, axis=-1, keepdims=True)).astype(jnp.bfloat16)
    attended = jnp.einsum("cqk,ckd->cqd", weights, value_rows, preferred_element_type=jnp.float32)
    return attended.astype(jnp.bfloat16)


def owner_layout(received, column, slot_count):
    source_count = column.shape[0]
    head_count = column.shape[1]
    upto_count = jnp.cumsum(column, axis=0)
    before_count = upto_count - column
    bucket_total = upto_count[-1]
    slot_range = jnp.arange(slot_count)
    source_dev = jnp.sum(upto_count[:, :, None] <= slot_range[None, None, :], axis=0)
    source_dev = jnp.minimum(source_dev, source_count - 1)
    source_range = jnp.arange(source_count)
    source_start = jnp.sum(
        jnp.where(source_dev[None] == source_range[:, None, None], before_count[:, :, None], 0),
        axis=0,
    )
    entry_row = jnp.clip(slot_range[None, :] - source_start, 0, received.shape[2] - 1)
    head_range = jnp.arange(head_count)
    layout = received[source_dev, head_range[:, None], entry_row]
    live = slot_range[None, :] < bucket_total[:, None]
    layout = jnp.where(live[..., None], layout, jnp.zeros((), layout.dtype))
    return (layout, live, before_count, bucket_total)


def tail_live(bucket_total, block_rows):
    return bucket_total[:, None] - block_rows + jnp.arange(block_rows)[None, :] >= 0


def last_rows(layout, bucket_total, block_rows):
    rank_index = bucket_total[:, None] - block_rows + jnp.arange(block_rows)[None, :]
    head_range = jnp.arange(layout.shape[0])
    rows = layout[head_range[:, None], jnp.maximum(rank_index, 0)]
    return jnp.where((rank_index >= 0)[..., None], rows, jnp.zeros((), rows.dtype))


def local_by_bucket(shared_qk, values, buckets, counts, w_out):
    tok_rows = shared_qk.shape[0]
    head_count = buckets.shape[1]
    head_dim = shared_qk.shape[1] // head_count
    seq_count = lax.axis_size("seq")
    capacity = 2 * tok_rows // seq_count
    slot_count = seq_count * capacity
    block_rows = BLOCK
    block_count = slot_count // block_rows
    own_index = lax.axis_index("seq")
    prev_index = (own_index + seq_count - 1) % seq_count
    head_range = jnp.arange(head_count)
    bucket_heads = buckets.T
    positions = jnp.arange(tok_rows)
    earlier = positions[None, :] < positions[:, None]
    same_bucket = bucket_heads[:, :, None] == bucket_heads[:, None, :]
    within = jnp.sum(same_bucket & earlier[None], axis=2)
    own_counts = lax.dynamic_index_in_dim(counts, own_index, 0, keepdims=False)
    own_starts = jnp.cumsum(own_counts, axis=1) - own_counts
    bucket_range = jnp.arange(seq_count)
    one_hot = bucket_heads[:, :, None] == bucket_range[None, None, :]
    token_start = jnp.sum(jnp.where(one_hot, own_starts[:, None, :], 0), axis=2)
    sorted_pos = token_start + within
    token_order = jnp.sum(
        jnp.where(sorted_pos[:, :, None] == positions[None, None, :], positions[None, :, None], 0),
        axis=1,
    )
    slot_range = jnp.arange(capacity)
    send_index = own_starts.T[:, :, None] + slot_range[None, None, :]
    filled = slot_range[None, None, :] < own_counts.T[:, :, None]
    token_pick = token_order[head_range[None, :, None], jnp.minimum(send_index, tok_rows - 1)]
    packed = jnp.concatenate(
        [
            shared_qk.reshape(tok_rows, head_count, head_dim),
            values.reshape(tok_rows, head_count, head_dim),
        ],
        axis=2,
    )
    outgoing = packed[token_pick, head_range[None, :, None]]
    outgoing = jnp.where(filled[..., None], outgoing, jnp.zeros((), outgoing.dtype))
    own_column = lax.dynamic_index_in_dim(counts, own_index, 2, keepdims=False)
    prev_column = lax.dynamic_index_in_dim(counts, prev_index, 2, keepdims=False)
    prev_total = jnp.sum(prev_column, axis=0)
    received = lax.all_to_all(outgoing, "seq", split_axis=0, concat_axis=0, tiled=True)
    layout, live, before_count, bucket_total = owner_layout(received, own_column, slot_count)
    tail_rows = last_rows(layout, bucket_total, block_rows)
    prev_rows = passed_along(tail_rows, "seq", 1)
    prev_live = tail_live(prev_total, block_rows)
    keys_all = jnp.concatenate([prev_rows, layout], axis=1)
    live_all = jnp.concatenate([prev_live, live], axis=1)
    window = jnp.concatenate(
        [
            keys_all[:, :slot_count].reshape(head_count, block_count, block_rows, 2 * head_dim),
            keys_all[:, block_rows:].reshape(head_count, block_count, block_rows, 2 * head_dim),
        ],
        axis=2,
    )
    window_live = jnp.concatenate(
        [
            live_all[:, :slot_count].reshape(head_count, block_count, block_rows),
            live_all[:, block_rows:].reshape(head_count, block_count, block_rows),
        ],
        axis=2,
    )
    queries = layout[..., :head_dim].reshape(head_count, block_count, block_rows, head_dim)
    attended = lax.map(
        lambda per_head: block_attention(per_head[0], per_head[1], per_head[2]),
        (queries, window, window_live),
    )
    out_layout = attended.reshape(head_count, slot_count, head_dim)
    back_index = before_count[:, :, None] + slot_range[None, None, :]
    back_filled = slot_range[None, None, :] < own_column[:, :, None]
    back_rows = out_layout[head_range[None, :, None], jnp.minimum(back_index, slot_count - 1)]
    back_rows = jnp.where(back_filled[..., None], back_rows, jnp.zeros((), back_rows.dtype))
    returned = lax.all_to_all(back_rows, "seq", split_axis=0, concat_axis=0, tiled=True)
    token_out = returned[buckets, head_range[None, :], within.T]
    token_out = token_out.reshape(tok_rows, head_count * head_dim)
    partial_sum = jnp.dot(token_out, w_out, preferred_element_type=jnp.float32)
    projected = lax.psum_scatter(partial_sum, "mp", scatter_dimension=1, tiled=True)
    return projected.astype(jnp.bfloat16)


PAD_ROWS = 8


def in_vmem(count):
    return [pl.BlockSpec(memory_space=pltpu.VMEM)] * count


def in_hbm(count):
    return [pl.BlockSpec(memory_space=pltpu.HBM)] * count


def stays_in_hbm(array):
    return pltpu.with_memory_space_constraint(array, pltpu.HBM)


def vmem_params(mebibytes):
    return pltpu.CompilerParams(vmem_limit_bytes=mebibytes * 2**20)


def moves(count):
    every = [(step, flip) for step in range(count // 2) for flip in range(2)]
    return sorted(every[1:], key=lambda move: (move[0] % 2, move[1], move[0]))


def moved(index, step, flip, count):
    return (index // 2 + step) % (count // 2) * 2 + (index % 2 + flip) % 2


def sent(block, step, flip):
    count = lax.axis_size("seq")
    return lax.ppermute(block, "seq", [(i, moved(i, step, flip, count)) for i in range(count)])


def block_copies(qk_hbm, value_hbm, head, qk_ref, value_ref, sems):
    head_dim = qk_ref.shape[1]
    columns = pl.ds(pl.multiple_of(head * head_dim, head_dim), head_dim)
    return [
        pltpu.make_async_copy(qk_hbm.at[:, columns], qk_ref, sems.at[0]),
        pltpu.make_async_copy(value_hbm.at[:, columns], value_ref, sems.at[1]),
    ]


def pack_kernel(bucket_hbm, qk_hbm, value_hbm, *refs):
    outs, (bucket_ref, bucket_sem, sems) = refs[:-3], refs[-3:]
    head_count = bucket_ref.shape[0]
    tok_rows = qk_hbm.shape[0]
    own = lax.axis_index("seq")
    heads = [moved(own, step, flip, head_count) for step, flip in moves(head_count)]
    fetch_buckets = pltpu.make_async_copy(bucket_hbm, bucket_ref, bucket_sem)
    fetch_buckets.start()
    copies = []
    for at, (head, out) in enumerate(zip(heads, outs)):
        qk_ref, value_ref = out.at[:tok_rows, :], out.at[tok_rows : 2 * tok_rows, :]
        copies += block_copies(qk_hbm, value_hbm, head, qk_ref, value_ref, sems.at[at])
    for copy in copies:
        copy.start()
    fetch_buckets.wait()
    for head, out in zip(heads, outs):
        bucket = bucket_ref[pl.ds(head, 1), :].astype(jnp.float32)
        out[2 * tok_rows :, :] = jnp.broadcast_to(bucket, (PAD_ROWS, tok_rows)).astype(out.dtype)
    for copy in copies:
        copy.wait()


def pack_blocks(bucket_heads, shared_qk, values):
    head_count, tok_rows = bucket_heads.shape
    head_dim = shared_qk.shape[1] // head_count
    block = pltpu.VMEM((2 * tok_rows + PAD_ROWS, head_dim), shared_qk.dtype)
    return pl.pallas_call(
        pack_kernel,
        in_specs=in_hbm(3),
        out_specs=in_vmem(head_count - 1),
        out_shape=[block] * (head_count - 1),
        scratch_shapes=[
            pltpu.VMEM(bucket_heads.shape, bucket_heads.dtype),
            pltpu.SemaphoreType.DMA(()),
            pltpu.SemaphoreType.DMA((head_count - 1, 2)),
        ],
        compiler_params=vmem_params(8),
        name="pack_blocks",
    )(*(stays_in_hbm(array) for array in (bucket_heads, shared_qk, values)))


def attend_kernel(bucket_hbm, qk_hbm, value_hbm, w_hbm, *refs, bucket_count, query_rows):
    source_count = bucket_hbm.shape[0]
    pair_count = source_count // 2
    block_refs, refs = refs[: source_count - 1], refs[source_count - 1 :]
    out_refs, refs = refs[:pair_count], refs[pair_count:]
    w_ref, query_ref, key_ref, value_ref = refs[:4]
    score_refs, term_refs = refs[4:7], refs[7:9]
    bucket_ref, sems = refs[9:]
    _, tok_rows, head_dim = out_refs[0].shape
    token_count = source_count * tok_rows
    own = lax.axis_index("seq")
    owners = [(-step % pair_count, (own + flip) % 2) for step, flip in (*moves(source_count), (0, 0))]
    last = slice(token_count - tok_rows, token_count)
    own_copies = block_copies(qk_hbm, value_hbm, own, key_ref.at[last, :head_dim], value_ref.at[last, :head_dim], sems)
    own_copies.append(pltpu.make_async_copy(bucket_hbm, bucket_ref, sems.at[2]))
    for copy in own_copies:
        copy.start()
    width = w_ref.shape[1]
    theirs = pl.multiple_of((1 - lax.axis_index("mp")) * width, width)
    fetch = pltpu.make_async_copy(w_hbm.at[:, pl.ds(theirs, width)], w_ref, sems.at[3])
    fetch.start()
    lane = lax.broadcasted_iota(jnp.int32, (tok_rows, head_dim), 1)

    def prepare(source):
        at = slice(source * tok_rows, (source + 1) * tok_rows)
        if source < source_count - 1:
            block_ref = block_refs[source]
            query_ref[at, :head_dim] = block_ref[:tok_rows, :]
            key_ref[at, :head_dim] = block_ref[:tok_rows, :]
            value_ref[at, :head_dim] = block_ref[tok_rows : 2 * tok_rows, :]
            row = block_ref[2 * tok_rows :, :].astype(jnp.float32)[:1]
        else:
            for copy in own_copies:
                copy.wait()
            query_ref[at, :head_dim] = key_ref[at, :head_dim]
            row = bucket_ref[pl.ds(own, 1), :].astype(jnp.float32)
        value_ref[at, head_dim:] = jnp.ones((tok_rows, head_dim), value_ref.dtype)
        bucket = jnp.broadcast_to(row, (head_dim, tok_rows)).T.astype(jnp.int32)
        following = jnp.where(bucket == bucket_count - 1, 0, bucket + 1)
        same = lane == bucket
        query_ref[at, head_dim:] = jnp.where(same, 1.0, 0.0).astype(query_ref.dtype)
        key_ref[at, head_dim:] = jnp.where(same | (lane == following), 0.0, MASKED).astype(key_ref.dtype)

    scale = 1.0 / math.sqrt(head_dim)
    strip = 16
    square = (tok_rows, tok_rows)
    itself = lax.broadcasted_iota(jnp.int32, square, 0) == lax.broadcasted_iota(jnp.int32, square, 1)

    def scores_of(block, score_ref, keys):
        score_ref[:, keys] = lax.dot_general(
            query_ref[block * query_rows : (block + 1) * query_rows, :],
            key_ref[keys, :],
            (((1,), (1,)), ((), ())),
            preferred_element_type=jnp.float32,
        )

    def replace_diagonal(block, score_ref):
        for at in range(0, query_rows, tok_rows):
            columns = slice(block * query_rows + at, block * query_rows + at + tok_rows)
            diagonal = score_ref[at : at + tok_rows, columns]
            score_ref[at : at + tok_rows, columns] = jnp.where(itself, SELF_SCORE / scale, diagonal)

    def terms_of(score_ref, term_ref):
        for at in range(0, query_rows, strip):
            scores = score_ref[at : at + strip, :]
            row_max = jnp.max(scores, axis=1, keepdims=True)
            terms = jnp.exp2((scores - row_max) * (scale * math.log2(math.e)))
            term_ref[at : at + strip, :] = terms.astype(term_ref.dtype)

    def attend_of(block, term_ref):
        both = jnp.dot(term_ref[...], value_ref[...], preferred_element_type=jnp.float32)
        attended = (both[:, :head_dim] / both[:, head_dim:]).astype(out_refs[0].dtype)
        for at in range(0, query_rows, tok_rows):
            step, which = owners[(block * query_rows + at) // tok_rows]
            out_refs[step][which] = attended[at : at + tok_rows]

    blocks = token_count // query_rows
    ahead = min(2, blocks)
    for tile in range(blocks):
        stop = (tile + 1) * query_rows
        for source in range(tile * query_rows // tok_rows, stop // tok_rows):
            prepare(source)
        for block in range(min(tile + 1, ahead)):
            keys = slice(0 if tile == block else tile * query_rows, stop)
            scores_of(block, score_refs[block], keys)
    for block in range(ahead):
        replace_diagonal(block, score_refs[block])
    for block in range(blocks):
        if block + ahead < blocks:
            scores_of(block + ahead, score_refs[(block + ahead) % 3], slice(0, token_count))
            replace_diagonal(block + ahead, score_refs[(block + ahead) % 3])
        terms_of(score_refs[block % 3], term_refs[block % 2])
        attend_of(block, term_refs[block % 2])
    fetch.wait()


def attend_head(bucket_heads, shared_qk, values, w_out, blocks, bucket_count):
    source_count, tok_rows = bucket_heads.shape
    head_dim = shared_qk.shape[1] // source_count
    token_count = source_count * tok_rows
    query_rows = 2 * tok_rows
    extended = pltpu.VMEM((token_count, 2 * head_dim), shared_qk.dtype)
    scores = pltpu.VMEM((query_rows, token_count), jnp.float32)
    terms = pltpu.VMEM((query_rows, token_count), shared_qk.dtype)
    return pl.pallas_call(
        functools.partial(attend_kernel, bucket_count=bucket_count, query_rows=query_rows),
        in_specs=in_hbm(4) + in_vmem(len(blocks)),
        out_specs=in_vmem(source_count // 2 + 1),
        out_shape=[pltpu.VMEM((2, tok_rows, head_dim), shared_qk.dtype)] * (source_count // 2)
        + [pltpu.VMEM((w_out.shape[0], w_out.shape[1] // 2), w_out.dtype)],
        scratch_shapes=[
            *(extended, extended, extended, scores, scores, scores, terms, terms),
            pltpu.VMEM(bucket_heads.shape, bucket_heads.dtype),
            pltpu.SemaphoreType.DMA((4,)),
        ],
        compiler_params=vmem_params(20),
        name="attend_head",
    )(*(stays_in_hbm(array) for array in (bucket_heads, shared_qk, values, w_out)), *blocks)


def gather_kernel(*refs):
    other = 1 - lax.axis_index("seq") % 2
    for at, pair_ref in enumerate(refs[:-1]):
        refs[-1][at] = pair_ref[other]


def gather_other(pairs):
    _, tok_rows, head_dim = pairs[0].shape
    return pl.pallas_call(
        gather_kernel,
        in_specs=in_vmem(len(pairs)),
        out_specs=in_vmem(1)[0],
        out_shape=pltpu.VMEM((len(pairs), tok_rows, head_dim), pairs[0].dtype),
        compiler_params=vmem_params(8),
        name="gather_other",
    )(*pairs)


def widen_kernel(*refs):
    pair_refs, (swapped_ref, w_ref, out_ref, wide_ref) = refs[:-4], refs[-4:]
    pair_count, _, head_dim = swapped_ref.shape
    own = lax.axis_index("seq")
    for step, pair_ref in enumerate(pair_refs):
        pair = (own // 2 + pair_count - step) % pair_count
        for rows, which in ((pair_ref[own % 2], own % 2), (swapped_ref[step], 1 - own % 2)):
            start = pl.multiple_of((pair * 2 + which) * head_dim, head_dim)
            wide_ref[:, pl.ds(start, head_dim)] = rows
    out_ref[...] = jnp.dot(
        wide_ref[...], w_ref[:, : out_ref.shape[1]], preferred_element_type=jnp.float32
    ).astype(out_ref.dtype)


def widen_and_project(pairs, swapped, w_theirs, columns):
    tok_rows = pairs[0].shape[1]
    return pl.pallas_call(
        widen_kernel,
        in_specs=in_vmem(len(pairs) + 2),
        out_specs=in_vmem(2),
        out_shape=[
            pltpu.VMEM((tok_rows, columns), swapped.dtype),
            pltpu.VMEM((tok_rows, w_theirs.shape[0]), swapped.dtype),
        ],
        compiler_params=vmem_params(16),
        name="widen_and_project",
    )(*pairs, swapped, w_theirs)


def theirs_kernel(wide_ref, w_ref, out_ref, *, start):
    out_ref[...] = jnp.dot(
        wide_ref[...], w_ref[:, start : start + out_ref.shape[1]], preferred_element_type=jnp.float32
    ).astype(out_ref.dtype)


def project_theirs(wide, w_theirs, start):
    return pl.pallas_call(
        functools.partial(theirs_kernel, start=start),
        in_specs=in_vmem(2),
        out_specs=in_vmem(1)[0],
        out_shape=pltpu.VMEM((wide.shape[0], w_theirs.shape[1] - start), wide.dtype),
        compiler_params=vmem_params(16),
        name="project_theirs",
    )(wide, w_theirs)


def ours_kernel(wide_ref, w_hbm, out_ref, w_ref, sems):
    chunks, _, columns = w_ref.shape
    start = pl.multiple_of(lax.axis_index("mp") * (chunks * columns), columns)
    copies = [
        pltpu.make_async_copy(w_hbm.at[:, pl.ds(start + chunk * columns, columns)], w_ref.at[chunk], sems.at[chunk])
        for chunk in range(chunks)
    ]
    for copy in copies:
        copy.start()
    for chunk, copy in enumerate(copies):
        copy.wait()
        out_ref[:, chunk * columns : (chunk + 1) * columns] = jnp.dot(
            wide_ref[...], w_ref[chunk], preferred_element_type=jnp.float32
        )


def project_ours(wide, w_out):
    tok_rows, depth = wide.shape
    chunks = 4
    columns = w_out.shape[1] // (2 * chunks)
    return pl.pallas_call(
        ours_kernel,
        in_specs=in_vmem(1) + in_hbm(1),
        out_specs=in_vmem(1)[0],
        out_shape=pltpu.VMEM((tok_rows, chunks * columns), jnp.float32),
        scratch_shapes=[
            pltpu.VMEM((chunks, depth, columns), w_out.dtype),
            pltpu.SemaphoreType.DMA((chunks,)),
        ],
        compiler_params=vmem_params(20),
        name="project_ours",
    )(wide, stays_in_hbm(w_out))


def add_kernel(ours_ref, *refs):
    out_ref = refs[-1]
    start = 0
    for theirs_ref in refs[:-1]:
        at = slice(start, start + theirs_ref.shape[1])
        start = at.stop
        out_ref[:, at] = (ours_ref[:, at] + theirs_ref[...].astype(jnp.float32)).astype(out_ref.dtype)


def add_parts(ours, theirs, dtype):
    return pl.pallas_call(
        add_kernel,
        in_specs=in_vmem(1 + len(theirs)),
        out_shape=jax.ShapeDtypeStruct(ours.shape, dtype),
        compiler_params=vmem_params(8),
        name="add_parts",
    )(ours, *theirs)


def local_by_head(shared_qk, values, buckets, counts, w_out):
    bucket_heads = buckets.T
    seq_count = lax.axis_size("seq")
    received = [
        sent(block, step, flip)
        for (step, flip), block in zip(moves(seq_count), pack_blocks(bucket_heads, shared_qk, values))
    ]
    *pairs, w_theirs = attend_head(bucket_heads, shared_qk, values, w_out, received, counts.shape[2])
    pairs = pairs[:1] + [sent(pair, step, 0) for step, pair in enumerate(pairs) if step]
    swapped = sent(gather_other(pairs), 0, 1)
    columns = w_theirs.shape[1] // 4
    first, wide = widen_and_project(pairs, swapped, w_theirs, columns)
    peers = [(0, 1), (1, 0)]
    arrived = [lax.ppermute(first, "mp", peers)]
    rest = project_theirs(wide, w_theirs, columns)
    arrived.append(lax.ppermute(rest, "mp", peers))
    ours = project_ours(wide, w_out)
    return add_parts(ours, arrived, shared_qk.dtype)


def local(shared_qk, values, buckets, counts, w_out):
    head_count = buckets.shape[1]
    seq_count = lax.axis_size("seq")
    one_head_each = head_count == seq_count and counts.shape[2] == seq_count and 2 < seq_count <= 128 and seq_count % 2 == 0
    if one_head_each and lax.axis_size("mp") == 2 and 2 * shared_qk.shape[0] <= BLOCK:
        return local_by_head(shared_qk, values, buckets, counts, w_out)
    return local_by_bucket(shared_qk, values, buckets, counts, w_out)


def solution(mesh):
    placed = (P("seq", "mp"), P("seq", "mp"), P("seq", "mp"), P(None, "mp", None), P("mp", None))
    return jax.shard_map(
        local, mesh=mesh, in_specs=placed, out_specs=P("seq", "mp"), check_vma=False
    )
```

profile of v0, /device:TPU:0, one launch (start us, length us, event | category | flops | bytes accessed | tf_op | source)
XLA Modules:
  0.0 71.9 jit_solution(181837368242632334)
XLA Ops:
  0.0 1.4 %pack_blocks.1 = (bf16[264,128]{1,0:T(8,128)(2,1)S(1)}, bf16[264,128]{1,0:T(8,128)(2,1)S(1)}, bf16[264,128]{1,0:T(8,128)(2,1)S(1)}, bf16[264,128]{1,0:T(8,128)(2...) custom-call(s32[16,128]{1,0:T(8,128)} %bitcast.1, ...), custom_call_target="tpu_custom_call" | custom-call | tf_op jit(solution)/shard_map/pack_blocks/pallas_call | solution.py:227
  1.4 3.1 %collective-permute-start = (bf16[264,128]{1,0:T(8,128)(2,1)S(1)}, bf16[264,128]{1,0:T(8,128)(2,1)S(1)}, u32[]{:S(2)}, u32[]{:S(2)}) collective-permute-start(bf16[264,128]{1,0:T(8,128)(2,1)S(1)} %get-tuple-element.31), channel_id=1, source_target_pairs={{0,8},{2,10},{4,12},{6,14},{8,16},{10,18},{12,20},{14,22},{16,24},... | collective-permute-start | bytes 202760 | tf_op jit(solution)/shard_map/ppermute | solution.py:189
  4.6 2.6 %collective-permute-start.1 = (bf16[264,128]{1,0:T(8,128)(2,1)S(1)}, bf16[264,128]{1,0:T(8,128)(2,1)S(1)}, u32[]{:S(2)}, u32[]{:S(2)}) collective-permute-start(bf16[264,128]{1,0:T(8,128)(2,1)S(1)} %get-tuple-element.32), channel_id=1, source_target_pairs={{0,16},{2,18},{4,20},{6,22},{8,24},{10,26},{12,28},{14,30},{16,0},... | collective-permute-start | bytes 202760 | tf_op jit(solution)/shard_map/ppermute | solution.py:189
  7.1 1.3 %collective-permute-start.2 = (bf16[264,128]{1,0:T(8,128)(2,1)S(1)}, bf16[264,128]{1,0:T(8,128)(2,1)S(1)}, u32[]{:S(2)}, u32[]{:S(2)}) collective-permute-start(bf16[264,128]{1,0:T(8,128)(2,1)S(1)} %get-tuple-element.33), channel_id=1, source_target_pairs={{0,24},{2,26},{4,28},{6,30},{8,0},{10,2},{12,4},{14,6},{16,8},{18,... | collective-permute-start | bytes 202760 | tf_op jit(solution)/shard_map/ppermute | solution.py:189
  8.5 0.8 %collective-permute-start.4 = (bf16[264,128]{1,0:T(8,128)(2,1)S(1)}, bf16[264,128]{1,0:T(8,128)(2,1)S(1)}, u32[]{:S(2)}, u32[]{:S(2)}) collective-permute-start(bf16[264,128]{1,0:T(8,128)(2,1)S(1)} %get-tuple-element.35), channel_id=1, source_target_pairs={{0,10},{2,8},{4,14},{6,12},{8,18},{10,16},{12,22},{14,20},{16,26},... | collective-permute-start | bytes 202760 | tf_op jit(solution)/shard_map/ppermute | solution.py:189
  9.3 2.4 %collective-permute-done.1.refs_1_ = bf16[264,128]{1,0:T(8,128)(2,1)S(1)} collective-permute-done((bf16[264,128]{1,0:T(8,128)(2,1)S(1)}, bf16[264,128]{1,0:T(8,128)(2,1)S(1)}, u32[]{:S(2)}, u32[]{:S(2)}) %collective-permute-start.1) | collective-permute-done | bytes 67616 | tf_op jit(solution)/shard_map/ppermute | solution.py:189
  12.1 1.5 %collective-permute-start.7 = (bf16[264,128]{1,0:T(8,128)(2,1)S(1)}, bf16[264,128]{1,0:T(8,128)(2,1)S(1)}, u32[]{:S(2)}, u32[]{:S(2)}) collective-permute-start(bf16[264,128]{1,0:T(8,128)(2,1)S(1)} %get-tuple-element.38), channel_id=1, source_target_pairs={{0,4},{2,6},{4,8},{6,10},{8,12},{10,14},{12,16},{14,18},{16,20},{1... | collective-permute-start | bytes 202760 | tf_op jit(solution)/shard_map/ppermute | solution.py:189
  13.6 2.0 %collective-permute-start.8 = (bf16[264,128]{1,0:T(8,128)(2,1)S(1)}, bf16[264,128]{1,0:T(8,128)(2,1)S(1)}, u32[]{:S(2)}, u32[]{:S(2)}) collective-permute-start(bf16[264,128]{1,0:T(8,128)(2,1)S(1)} %get-tuple-element.39), channel_id=1, source_target_pairs={{0,12},{2,14},{4,16},{6,18},{8,20},{10,22},{12,24},{14,26},{16,28}... | collective-permute-start | bytes 202760 | tf_op jit(solution)/shard_map/ppermute | solution.py:189
  15.7 1.8 %collective-permute-start.9 = (bf16[264,128]{1,0:T(8,128)(2,1)S(1)}, bf16[264,128]{1,0:T(8,128)(2,1)S(1)}, u32[]{:S(2)}, u32[]{:S(2)}) collective-permute-start(bf16[264,128]{1,0:T(8,128)(2,1)S(1)} %get-tuple-element.40), channel_id=1, source_target_pairs={{0,20},{2,22},{4,24},{6,26},{8,28},{10,30},{12,0},{14,2},{16,4},{1... | collective-permute-start | bytes 202760 | tf_op jit(solution)/shard_map/ppermute | solution.py:189
  17.5 3.3 %collective-permute-start.10 = (bf16[264,128]{1,0:T(8,128)(2,1)S(1)}, bf16[264,128]{1,0:T(8,128)(2,1)S(1)}, u32[]{:S(2)}, u32[]{:S(2)}) collective-permute-start(bf16[264,128]{1,0:T(8,128)(2,1)S(1)} %get-tuple-element.41), channel_id=1, source_target_pairs={{0,28},{2,30},{4,0},{6,2},{8,4},{10,6},{12,8},{14,10},{16,12},{18,... | collective-permute-start | bytes 202760 | tf_op jit(solution)/shard_map/ppermute | solution.py:189
  20.8 1.0 %collective-permute-start.11 = (bf16[264,128]{1,0:T(8,128)(2,1)S(1)}, bf16[264,128]{1,0:T(8,128)(2,1)S(1)}, u32[]{:S(2)}, u32[]{:S(2)}) collective-permute-start(bf16[264,128]{1,0:T(8,128)(2,1)S(1)} %get-tuple-element.42), channel_id=1, source_target_pairs={{0,6},{2,4},{4,10},{6,8},{8,14},{10,12},{12,18},{14,16},{16,22},{1... | collective-permute-start | bytes 202760 | tf_op jit(solution)/shard_map/ppermute | solution.py:189
  22.2 2.2 %collective-permute-done.8.refs_8_ = bf16[264,128]{1,0:T(8,128)(2,1)S(1)} collective-permute-done((bf16[264,128]{1,0:T(8,128)(2,1)S(1)}, bf16[264,128]{1,0:T(8,128)(2,1)S(1)}, u32[]{:S(2)}, u32[]{:S(2)}) %collective-permute-start.8) | collective-permute-done | bytes 67616 | tf_op jit(solution)/shard_map/ppermute | solution.py:189
  24.4 0.9 %collective-permute-start.13 = (bf16[264,128]{1,0:T(8,128)(2,1)S(1)}, bf16[264,128]{1,0:T(8,128)(2,1)S(1)}, u32[]{:S(2)}, u32[]{:S(2)}) collective-permute-start(bf16[264,128]{1,0:T(8,128)(2,1)S(1)} %get-tuple-element.44), channel_id=1, source_target_pairs={{0,22},{2,20},{4,26},{6,24},{8,30},{10,28},{12,2},{14,0},{16,6},{1... | collective-permute-start | bytes 202760 | tf_op jit(solution)/shard_map/ppermute | solution.py:189
  25.3 2.6 %collective-permute-start.14 = (bf16[264,128]{1,0:T(8,128)(2,1)S(1)}, bf16[264,128]{1,0:T(8,128)(2,1)S(1)}, u32[]{:S(2)}, u32[]{:S(2)}) collective-permute-start(bf16[264,128]{1,0:T(8,128)(2,1)S(1)} %get-tuple-element.45), channel_id=1, source_target_pairs={{0,30},{2,28},{4,2},{6,0},{8,6},{10,4},{12,10},{14,8},{16,14},{18,... | collective-permute-start | bytes 202760 | tf_op jit(solution)/shard_map/ppermute | solution.py:189
  27.9 2.8 %collective-permute-done.12.refs_12_ = bf16[264,128]{1,0:T(8,128)(2,1)S(1)} collective-permute-done((bf16[264,128]{1,0:T(8,128)(2,1)S(1)}, bf16[264,128]{1,0:T(8,128)(2,1)S(1)}, u32[]{:S(2)}, u32[]{:S(2)}) %collective-permute-start.12) | collective-permute-done | bytes 67616 | tf_op jit(solution)/shard_map/ppermute | solution.py:189
  30.8 0.8 %collective-permute-done.13.refs_13_ = bf16[264,128]{1,0:T(8,128)(2,1)S(1)} collective-permute-done((bf16[264,128]{1,0:T(8,128)(2,1)S(1)}, bf16[264,128]{1,0:T(8,128)(2,1)S(1)}, u32[]{:S(2)}, u32[]{:S(2)}) %collective-permute-start.13) | collective-permute-done | bytes 67616 | tf_op jit(solution)/shard_map/ppermute | solution.py:189
  31.6 1.4 %collective-permute-done.14.refs_14_ = bf16[264,128]{1,0:T(8,128)(2,1)S(1)} collective-permute-done((bf16[264,128]{1,0:T(8,128)(2,1)S(1)}, bf16[264,128]{1,0:T(8,128)(2,1)S(1)}, u32[]{:S(2)}, u32[]{:S(2)}) %collective-permute-start.14) | collective-permute-done | bytes 67616 | tf_op jit(solution)/shard_map/ppermute | solution.py:189
  33.0 6.4 %attend_head.1 = (bf16[2,128,128]{2,1,0:T(8,128)(2,1)S(1)}, bf16[2,128,128]{2,1,0:T(8,128)(2,1)S(1)}, bf16[2,128,128]{2,1,0:T(8,128)(2,1)S(1)}, bf16[2,128,128]{...) custom-call(s32[16,128]{1,0:T(8,128)} %bitcast.2, ...), custom_call_target="tpu_custom_call" | custom-call | tf_op jit(solution)/shard_map/attend_head/pallas_call | solution.py:346
  39.3 1.1 %collective-permute-start.15 = (bf16[2,128,128]{2,1,0:T(8,128)(2,1)S(1)}, bf16[2,128,128]{2,1,0:T(8,128)(2,1)S(1)}, u32[]{:S(2)}, u32[]{:S(2)}) collective-permute-start(bf16[2,128,128]{2,1,0:T(8,128)(2,1)S(1)} %get-tuple-element.47), channel_id=1, source_target_pairs={{0,4},{2,6},{4,8},{6,10},{8,12},{10,14},{12,16},{14,18},{16,20},{1... | collective-permute-start | bytes 196616 | tf_op jit(solution)/shard_map/ppermute | solution.py:189
  40.9 2.4 %collective-permute-start.17 = (bf16[2,128,128]{2,1,0:T(8,128)(2,1)S(1)}, bf16[2,128,128]{2,1,0:T(8,128)(2,1)S(1)}, u32[]{:S(2)}, u32[]{:S(2)}) collective-permute-start(bf16[2,128,128]{2,1,0:T(8,128)(2,1)S(1)} %get-tuple-element.49), channel_id=1, source_target_pairs={{0,12},{2,14},{4,16},{6,18},{8,20},{10,22},{12,24},{14,26},{16,28}... | collective-permute-start | bytes 196616 | tf_op jit(solution)/shard_map/ppermute | solution.py:189
  43.3 1.5 %collective-permute-start.18 = (bf16[2,128,128]{2,1,0:T(8,128)(2,1)S(1)}, bf16[2,128,128]{2,1,0:T(8,128)(2,1)S(1)}, u32[]{:S(2)}, u32[]{:S(2)}) collective-permute-start(bf16[2,128,128]{2,1,0:T(8,128)(2,1)S(1)} %get-tuple-element.50), channel_id=1, source_target_pairs={{0,16},{2,18},{4,20},{6,22},{8,24},{10,26},{12,28},{14,30},{16,0},... | collective-permute-start | bytes 196616 | tf_op jit(solution)/shard_map/ppermute | solution.py:189
  44.8 2.4 %collective-permute-start.19 = (bf16[2,128,128]{2,1,0:T(8,128)(2,1)S(1)}, bf16[2,128,128]{2,1,0:T(8,128)(2,1)S(1)}, u32[]{:S(2)}, u32[]{:S(2)}) collective-permute-start(bf16[2,128,128]{2,1,0:T(8,128)(2,1)S(1)} %get-tuple-element.51), channel_id=1, source_target_pairs={{0,20},{2,22},{4,24},{6,26},{8,28},{10,30},{12,0},{14,2},{16,4},{1... | collective-permute-start | bytes 196616 | tf_op jit(solution)/shard_map/ppermute | solution.py:189
  47.2 0.9 %collective-permute-start.20 = (bf16[2,128,128]{2,1,0:T(8,128)(2,1)S(1)}, bf16[2,128,128]{2,1,0:T(8,128)(2,1)S(1)}, u32[]{:S(2)}, u32[]{:S(2)}) collective-permute-start(bf16[2,128,128]{2,1,0:T(8,128)(2,1)S(1)} %get-tuple-element.52), channel_id=1, source_target_pairs={{0,24},{2,26},{4,28},{6,30},{8,0},{10,2},{12,4},{14,6},{16,8},{18,... | collective-permute-start | bytes 196616 | tf_op jit(solution)/shard_map/ppermute | solution.py:189
  48.1 1.8 %collective-permute-start.21 = (bf16[2,128,128]{2,1,0:T(8,128)(2,1)S(1)}, bf16[2,128,128]{2,1,0:T(8,128)(2,1)S(1)}, u32[]{:S(2)}, u32[]{:S(2)}) collective-permute-start(bf16[2,128,128]{2,1,0:T(8,128)(2,1)S(1)} %get-tuple-element.53), channel_id=1, source_target_pairs={{0,28},{2,30},{4,0},{6,2},{8,4},{10,6},{12,8},{14,10},{16,12},{18,... | collective-permute-start | bytes 196616 | tf_op jit(solution)/shard_map/ppermute | solution.py:189
  49.9 2.0 %collective-permute-done.17.refs_3_ = bf16[2,128,128]{2,1,0:T(8,128)(2,1)S(1)} collective-permute-done((bf16[2,128,128]{2,1,0:T(8,128)(2,1)S(1)}, bf16[2,128,128]{2,1,0:T(8,128)(2,1)S(1)}, u32[]{:S(2)}, u32[]{:S(2)}) %collective-permute-start.17) | collective-permute-done | bytes 65568 | tf_op jit(solution)/shard_map/ppermute | solution.py:189
  52.3 1.6 %collective-permute-done.20.refs_6_ = bf16[2,128,128]{2,1,0:T(8,128)(2,1)S(1)} collective-permute-done((bf16[2,128,128]{2,1,0:T(8,128)(2,1)S(1)}, bf16[2,128,128]{2,1,0:T(8,128)(2,1)S(1)}, u32[]{:S(2)}, u32[]{:S(2)}) %collective-permute-start.20) | collective-permute-done | bytes 65568 | tf_op jit(solution)/shard_map/ppermute | solution.py:189
  53.9 1.5 %collective-permute-done.22.refs_8_ = bf16[8,128,128]{2,1,0:T(8,128)(2,1)S(1)} collective-permute-done((bf16[8,128,128]{2,1,0:T(8,128)(2,1)S(1)}, bf16[8,128,128]{2,1,0:T(8,128)(2,1)S(1)}, u32[]{:S(2)}, u32[]{:S(2)}) %collective-permute-start.22) | collective-permute-done | bytes 262176 | tf_op jit(solution)/shard_map/ppermute | solution.py:189
  56.0 1.0 %project_theirs.1 = bf16[128,1536]{1,0:T(8,128)(2,1)S(1)} custom-call(bf16[128,2048]{1,0:T(8,128)(2,1)S(1)} %get-tuple-element.55.wide_ref, bf16[2048,2048]{1,0:T(8,128)(2,1)S(1)} %get-tuple-element.54.refs_9_.w_ref), custom_call_target="tpu_custom_call" | custom-call | tf_op jit(solution)/shard_map/project_theirs/pallas_call | solution.py:416
  57.0 1.5 %collective-permute-start.24 = (bf16[128,1536]{1,0:T(8,128)(2,1)S(1)}, bf16[128,1536]{1,0:T(8,128)(2,1)S(1)}, u32[]{:S(2)}, u32[]{:S(2)}) collective-permute-start(bf16[128,1536]{1,0:T(8,128)(2,1)S(1)} %project_theirs.1), channel_id=1, source_target_pairs={{0,1},{1,0},{2,3},{3,2},{4,5},{5,4},{6,7},{7,6},{8,9},{9,8},{10,11... | collective-permute-start | bytes 1179656 | tf_op jit(solution)/shard_map/ppermute | solution.py:494
  59.1 4.0 %project_ours.1.ours_ref = f32[128,2048]{1,0:T(8,128)S(1)} custom-call(bf16[128,2048]{1,0:T(8,128)(2,1)S(1)} %get-tuple-element.55.wide_ref, bf16[2048,4096]{1,0:T(8,128)(2,1)} %w_hbm.3), custom_call_target="tpu_custom_call" | custom-call | tf_op jit(solution)/shard_map/project_ours/pallas_call | solution.py:446
  63.1 7.9 %collective-permute-done.23.refs_0_ = bf16[128,512]{1,0:T(8,128)(2,1)S(1)} collective-permute-done((bf16[128,512]{1,0:T(8,128)(2,1)S(1)}, bf16[128,512]{1,0:T(8,128)(2,1)S(1)}, u32[]{:S(2)}, u32[]{:S(2)}) %collective-permute-start.23) | collective-permute-done | bytes 131104 | tf_op jit(solution)/shard_map/ppermute | solution.py:492
  71.1 0.9 %add_parts.1 = bf16[128,2048]{1,0:T(8,128)(2,1)} custom-call(f32[128,2048]{1,0:T(8,128)S(1)} %project_ours.1.ours_ref, bf16[128,512]{1,0:T(8,128)(2,1)S(1)} %collective-permute-done.23.refs_0_, bf16[128,1536]{1,0:T(8,128)(2,1)S(1)} %collective-permute-done.24.refs_1_), custom_call_target="tpu_custom_call" | custom-call | tf_op jit(solution)/shard_map/add_parts/pallas_call | solution.py:470
  (25 shorter events, 2.8 us)
Async XLA Ops:
  1.4 7.8 %collective-permute-start = (bf16[264,128]{1,0:T(8,128)(2,1)S(1)}, bf16[264,128]{1,0:T(8,128)(2,1)S(1)}, u32[]{:S(2)}, u32[]{:S(2)}) collective-permute-start(bf16[264,128]{1,0:T(8,128)(2,1)S(1)} %get-tuple-element.31), channel_id=1, source_target_pairs={{0,8},{2,10},{4,12},{6,14},{8,16},{10,18},{12,20},{14,22},{16,24},... | collective-permute-start | bytes 202760 | tf_op jit(solution)/shard_map/ppermute | solution.py:189
  4.6 7.2 %collective-permute-start.1 = (bf16[264,128]{1,0:T(8,128)(2,1)S(1)}, bf16[264,128]{1,0:T(8,128)(2,1)S(1)}, u32[]{:S(2)}, u32[]{:S(2)}) collective-permute-start(bf16[264,128]{1,0:T(8,128)(2,1)S(1)} %get-tuple-element.32), channel_id=1, source_target_pairs={{0,16},{2,18},{4,20},{6,22},{8,24},{10,26},{12,28},{14,30},{16,0},... | collective-permute-start | bytes 202760 | tf_op jit(solution)/shard_map/ppermute | solution.py:189
  7.1 5.0 %collective-permute-start.2 = (bf16[264,128]{1,0:T(8,128)(2,1)S(1)}, bf16[264,128]{1,0:T(8,128)(2,1)S(1)}, u32[]{:S(2)}, u32[]{:S(2)}) collective-permute-start(bf16[264,128]{1,0:T(8,128)(2,1)S(1)} %get-tuple-element.33), channel_id=1, source_target_pairs={{0,24},{2,26},{4,28},{6,30},{8,0},{10,2},{12,4},{14,6},{16,8},{18,... | collective-permute-start | bytes 202760 | tf_op jit(solution)/shard_map/ppermute | solution.py:189
  8.5 5.1 %collective-permute-start.3 = (bf16[264,128]{1,0:T(8,128)(2,1)S(1)}, bf16[264,128]{1,0:T(8,128)(2,1)S(1)}, u32[]{:S(2)}, u32[]{:S(2)}) collective-permute-start(bf16[264,128]{1,0:T(8,128)(2,1)S(1)} %get-tuple-element.34), channel_id=1, source_target_pairs={{0,2},{2,0},{4,6},{6,4},{8,10},{10,8},{12,14},{14,12},{16,18},{18,... | collective-permute-start | bytes 202760 | tf_op jit(solution)/shard_map/ppermute | solution.py:189
  8.5 7.2 %collective-permute-start.4 = (bf16[264,128]{1,0:T(8,128)(2,1)S(1)}, bf16[264,128]{1,0:T(8,128)(2,1)S(1)}, u32[]{:S(2)}, u32[]{:S(2)}) collective-permute-start(bf16[264,128]{1,0:T(8,128)(2,1)S(1)} %get-tuple-element.35), channel_id=1, source_target_pairs={{0,10},{2,8},{4,14},{6,12},{8,18},{10,16},{12,22},{14,20},{16,26},... | collective-permute-start | bytes 202760 | tf_op jit(solution)/shard_map/ppermute | solution.py:189
  9.3 8.2 %collective-permute-start.5 = (bf16[264,128]{1,0:T(8,128)(2,1)S(1)}, bf16[264,128]{1,0:T(8,128)(2,1)S(1)}, u32[]{:S(2)}, u32[]{:S(2)}) collective-permute-start(bf16[264,128]{1,0:T(8,128)(2,1)S(1)} %get-tuple-element.36), channel_id=1, source_target_pairs={{0,18},{2,16},{4,22},{6,20},{8,26},{10,24},{12,30},{14,28},{16,2},... | collective-permute-start | bytes 202760 | tf_op jit(solution)/shard_map/ppermute | solution.py:189
  11.7 9.0 %collective-permute-start.6 = (bf16[264,128]{1,0:T(8,128)(2,1)S(1)}, bf16[264,128]{1,0:T(8,128)(2,1)S(1)}, u32[]{:S(2)}, u32[]{:S(2)}) collective-permute-start(bf16[264,128]{1,0:T(8,128)(2,1)S(1)} %get-tuple-element.37), channel_id=1, source_target_pairs={{0,26},{2,24},{4,30},{6,28},{8,2},{10,0},{12,6},{14,4},{16,10},{18... | collective-permute-start | bytes 202760 | tf_op jit(solution)/shard_map/ppermute | solution.py:189
  12.1 9.7 %collective-permute-start.7 = (bf16[264,128]{1,0:T(8,128)(2,1)S(1)}, bf16[264,128]{1,0:T(8,128)(2,1)S(1)}, u32[]{:S(2)}, u32[]{:S(2)}) collective-permute-start(bf16[264,128]{1,0:T(8,128)(2,1)S(1)} %get-tuple-element.38), channel_id=1, source_target_pairs={{0,4},{2,6},{4,8},{6,10},{8,12},{10,14},{12,16},{14,18},{16,20},{1... | collective-permute-start | bytes 202760 | tf_op jit(solution)/shard_map/ppermute | solution.py:189
  13.6 10.7 %collective-permute-start.8 = (bf16[264,128]{1,0:T(8,128)(2,1)S(1)}, bf16[264,128]{1,0:T(8,128)(2,1)S(1)}, u32[]{:S(2)}, u32[]{:S(2)}) collective-permute-start(bf16[264,128]{1,0:T(8,128)(2,1)S(1)} %get-tuple-element.39), channel_id=1, source_target_pairs={{0,12},{2,14},{4,16},{6,18},{8,20},{10,22},{12,24},{14,26},{16,28}... | collective-permute-start | bytes 202760 | tf_op jit(solution)/shard_map/ppermute | solution.py:189
  15.7 9.7 %collective-permute-start.9 = (bf16[264,128]{1,0:T(8,128)(2,1)S(1)}, bf16[264,128]{1,0:T(8,128)(2,1)S(1)}, u32[]{:S(2)}, u32[]{:S(2)}) collective-permute-start(bf16[264,128]{1,0:T(8,128)(2,1)S(1)} %get-tuple-element.40), channel_id=1, source_target_pairs={{0,20},{2,22},{4,24},{6,26},{8,28},{10,30},{12,0},{14,2},{16,4},{1... | collective-permute-start | bytes 202760 | tf_op jit(solution)/shard_map/ppermute | solution.py:189
  17.5 10.5 %collective-permute-start.10 = (bf16[264,128]{1,0:T(8,128)(2,1)S(1)}, bf16[264,128]{1,0:T(8,128)(2,1)S(1)}, u32[]{:S(2)}, u32[]{:S(2)}) collective-permute-start(bf16[264,128]{1,0:T(8,128)(2,1)S(1)} %get-tuple-element.41), channel_id=1, source_target_pairs={{0,28},{2,30},{4,0},{6,2},{8,4},{10,6},{12,8},{14,10},{16,12},{18,... | collective-permute-start | bytes 202760 | tf_op jit(solution)/shard_map/ppermute | solution.py:189
  20.8 7.2 %collective-permute-start.11 = (bf16[264,128]{1,0:T(8,128)(2,1)S(1)}, bf16[264,128]{1,0:T(8,128)(2,1)S(1)}, u32[]{:S(2)}, u32[]{:S(2)}) collective-permute-start(bf16[264,128]{1,0:T(8,128)(2,1)S(1)} %get-tuple-element.42), channel_id=1, source_target_pairs={{0,6},{2,4},{4,10},{6,8},{8,14},{10,12},{12,18},{14,16},{16,22},{1... | collective-permute-start | bytes 202760 | tf_op jit(solution)/shard_map/ppermute | solution.py:189
  21.8 9.0 %collective-permute-start.12 = (bf16[264,128]{1,0:T(8,128)(2,1)S(1)}, bf16[264,128]{1,0:T(8,128)(2,1)S(1)}, u32[]{:S(2)}, u32[]{:S(2)}) collective-permute-start(bf16[264,128]{1,0:T(8,128)(2,1)S(1)} %get-tuple-element.43), channel_id=1, source_target_pairs={{0,14},{2,12},{4,18},{6,16},{8,22},{10,20},{12,26},{14,24},{16,30}... | collective-permute-start | bytes 202760 | tf_op jit(solution)/shard_map/ppermute | solution.py:189
  24.4 7.2 %collective-permute-start.13 = (bf16[264,128]{1,0:T(8,128)(2,1)S(1)}, bf16[264,128]{1,0:T(8,128)(2,1)S(1)}, u32[]{:S(2)}, u32[]{:S(2)}) collective-permute-start(bf16[264,128]{1,0:T(8,128)(2,1)S(1)} %get-tuple-element.44), channel_id=1, source_target_pairs={{0,22},{2,20},{4,26},{6,24},{8,30},{10,28},{12,2},{14,0},{16,6},{1... | collective-permute-start | bytes 202760 | tf_op jit(solution)/shard_map/ppermute | solution.py:189
  25.3 7.6 %collective-permute-start.14 = (bf16[264,128]{1,0:T(8,128)(2,1)S(1)}, bf16[264,128]{1,0:T(8,128)(2,1)S(1)}, u32[]{:S(2)}, u32[]{:S(2)}) collective-permute-start(bf16[264,128]{1,0:T(8,128)(2,1)S(1)} %get-tuple-element.45), channel_id=1, source_target_pairs={{0,30},{2,28},{4,2},{6,0},{8,6},{10,4},{12,10},{14,8},{16,14},{18,... | collective-permute-start | bytes 202760 | tf_op jit(solution)/shard_map/ppermute | solution.py:189
  39.3 7.9 %collective-permute-start.15 = (bf16[2,128,128]{2,1,0:T(8,128)(2,1)S(1)}, bf16[2,128,128]{2,1,0:T(8,128)(2,1)S(1)}, u32[]{:S(2)}, u32[]{:S(2)}) collective-permute-start(bf16[2,128,128]{2,1,0:T(8,128)(2,1)S(1)} %get-tuple-element.47), channel_id=1, source_target_pairs={{0,4},{2,6},{4,8},{6,10},{8,12},{10,14},{12,16},{14,18},{16,20},{1... | collective-permute-start | bytes 196616 | tf_op jit(solution)/shard_map/ppermute | solution.py:189
  40.4 7.7 %collective-permute-start.16 = (bf16[2,128,128]{2,1,0:T(8,128)(2,1)S(1)}, bf16[2,128,128]{2,1,0:T(8,128)(2,1)S(1)}, u32[]{:S(2)}, u32[]{:S(2)}) collective-permute-start(bf16[2,128,128]{2,1,0:T(8,128)(2,1)S(1)} %get-tuple-element.48), channel_id=1, source_target_pairs={{0,8},{2,10},{4,12},{6,14},{8,16},{10,18},{12,20},{14,22},{16,24},... | collective-permute-start | bytes 196616 | tf_op jit(solution)/shard_map/ppermute | solution.py:189
  40.9 11.0 %collective-permute-start.17 = (bf16[2,128,128]{2,1,0:T(8,128)(2,1)S(1)}, bf16[2,128,128]{2,1,0:T(8,128)(2,1)S(1)}, u32[]{:S(2)}, u32[]{:S(2)}) collective-permute-start(bf16[2,128,128]{2,1,0:T(8,128)(2,1)S(1)} %get-tuple-element.49), channel_id=1, source_target_pairs={{0,12},{2,14},{4,16},{6,18},{8,20},{10,22},{12,24},{14,26},{16,28}... | collective-permute-start | bytes 196616 | tf_op jit(solution)/shard_map/ppermute | solution.py:189
  43.3 8.9 %collective-permute-start.18 = (bf16[2,128,128]{2,1,0:T(8,128)(2,1)S(1)}, bf16[2,128,128]{2,1,0:T(8,128)(2,1)S(1)}, u32[]{:S(2)}, u32[]{:S(2)}) collective-permute-start(bf16[2,128,128]{2,1,0:T(8,128)(2,1)S(1)} %get-tuple-element.50), channel_id=1, source_target_pairs={{0,16},{2,18},{4,20},{6,22},{8,24},{10,26},{12,28},{14,30},{16,0},... | collective-permute-start | bytes 196616 | tf_op jit(solution)/shard_map/ppermute | solution.py:189
  44.8 7.4 %collective-permute-start.19 = (bf16[2,128,128]{2,1,0:T(8,128)(2,1)S(1)}, bf16[2,128,128]{2,1,0:T(8,128)(2,1)S(1)}, u32[]{:S(2)}, u32[]{:S(2)}) collective-permute-start(bf16[2,128,128]{2,1,0:T(8,128)(2,1)S(1)} %get-tuple-element.51), channel_id=1, source_target_pairs={{0,20},{2,22},{4,24},{6,26},{8,28},{10,30},{12,0},{14,2},{16,4},{1... | collective-permute-start | bytes 196616 | tf_op jit(solution)/shard_map/ppermute | solution.py:189
  47.2 6.6 %collective-permute-start.20 = (bf16[2,128,128]{2,1,0:T(8,128)(2,1)S(1)}, bf16[2,128,128]{2,1,0:T(8,128)(2,1)S(1)}, u32[]{:S(2)}, u32[]{:S(2)}) collective-permute-start(bf16[2,128,128]{2,1,0:T(8,128)(2,1)S(1)} %get-tuple-element.52), channel_id=1, source_target_pairs={{0,24},{2,26},{4,28},{6,30},{8,0},{10,2},{12,4},{14,6},{16,8},{18,... | collective-permute-start | bytes 196616 | tf_op jit(solution)/shard_map/ppermute | solution.py:189
  48.1 5.7 %collective-permute-start.21 = (bf16[2,128,128]{2,1,0:T(8,128)(2,1)S(1)}, bf16[2,128,128]{2,1,0:T(8,128)(2,1)S(1)}, u32[]{:S(2)}, u32[]{:S(2)}) collective-permute-start(bf16[2,128,128]{2,1,0:T(8,128)(2,1)S(1)} %get-tuple-element.53), channel_id=1, source_target_pairs={{0,28},{2,30},{4,0},{6,2},{8,4},{10,6},{12,8},{14,10},{16,12},{18,... | collective-permute-start | bytes 196616 | tf_op jit(solution)/shard_map/ppermute | solution.py:189
  53.8 1.6 %collective-permute-start.22 = (bf16[8,128,128]{2,1,0:T(8,128)(2,1)S(1)}, bf16[8,128,128]{2,1,0:T(8,128)(2,1)S(1)}, u32[]{:S(2)}, u32[]{:S(2)}) collective-permute-start(bf16[8,128,128]{2,1,0:T(8,128)(2,1)S(1)} %gather_other.1), channel_id=1, source_target_pairs={{0,2},{2,0},{4,6},{6,4},{8,10},{10,8},{12,14},{14,12},{16,18},{18,... | collective-permute-start | bytes 786440 | tf_op jit(solution)/shard_map/ppermute | solution.py:189
  57.0 14.0 %collective-permute-start.24 = (bf16[128,1536]{1,0:T(8,128)(2,1)S(1)}, bf16[128,1536]{1,0:T(8,128)(2,1)S(1)}, u32[]{:S(2)}, u32[]{:S(2)}) collective-permute-start(bf16[128,1536]{1,0:T(8,128)(2,1)S(1)} %project_theirs.1), channel_id=1, source_target_pairs={{0,1},{1,0},{2,3},{3,2},{4,5},{5,4},{6,7},{7,6},{8,9},{9,8},{10,11... | collective-permute-start | bytes 1179656 | tf_op jit(solution)/shard_map/ppermute | solution.py:494
  58.6 12.5 %collective-permute-start.23 = (bf16[128,512]{1,0:T(8,128)(2,1)S(1)}, bf16[128,512]{1,0:T(8,128)(2,1)S(1)}, u32[]{:S(2)}, u32[]{:S(2)}) collective-permute-start(bf16[128,512]{1,0:T(8,128)(2,1)S(1)} %get-tuple-element.56), channel_id=1, source_target_pairs={{0,1},{1,0},{2,3},{3,2},{4,5},{5,4},{6,7},{7,6},{8,9},{9,8},{10,11... | collective-permute-start | bytes 393224 | tf_op jit(solution)/shard_map/ppermute | solution.py:492
where the time goes:
time: 72.2 us; the launch traced here: 71.9 us
  starting transfers between devices  34.5 us (48%)
  waiting for transfers between devices  23 us (32%)
  Pallas kernels  14.3 us (20%)
    ppermute x23, starting transfers between devices, sent(): lax.ppermute(block, 'seq', [(i, moved(i, step, flip, count)) for i in ran...  32.4 us
    ppermute x23, waiting for transfers between devices, sent(): lax.ppermute(block, 'seq', [(i, moved(i, step, flip, count)) for i in ran...  15.1 us
    ppermute x1, waiting for transfers between devices, local_by_head(): arrived = [lax.ppermute(first, 'mp', peers)]  7.93 us
    pallas_call x1, Pallas kernels, attend_head(): pl.pallas_call(functools.partial(attend_kernel, bucket_count=bucket_count...  6.37 us
    pallas_call x1, Pallas kernels, project_ours(): pl.pallas_call(ours_kernel, in_specs=in_vmem(1) + in_hbm(1), out_specs=in...  3.99 us
    ppermute x1, starting transfers between devices, local_by_head(): arrived.append(lax.ppermute(rest, 'mp', peers))  1.54 us
  transfers between devices with their start and end apart: 25, of which 10 were waited for; matrix products, arithmetic and copies ran while one was open for 0% of the time, Pallas kernels for 6%

commit v1 on v0

--- a/solution.py
+++ b/solution.py
@@ -157,6 +157,7 @@
 
 
 PAD_ROWS = 8
+FETCHES = 8
 
 
 def in_vmem(count):
@@ -239,67 +240,108 @@
     )(*(stays_in_hbm(array) for array in (bucket_heads, shared_qk, values)))
 
 
-def attend_kernel(bucket_hbm, qk_hbm, value_hbm, w_hbm, *refs, bucket_count, query_rows):
-    source_count = bucket_hbm.shape[0]
+def extend(block, bucket_row, query_ref, key_ref, value_ref, rows, bucket_count):
+    qk, value = block
+    tok_rows, head_dim = value.shape
+    lane = lax.broadcasted_iota(jnp.int32, (tok_rows, head_dim), 1)
+    query_ref[rows, :head_dim] = qk
+    key_ref[rows, :head_dim] = qk
+    value_ref[rows, :head_dim] = value
+    value_ref[rows, head_dim:] = jnp.ones((tok_rows, head_dim), value_ref.dtype)
+    bucket = jnp.broadcast_to(bucket_row, (head_dim, tok_rows)).T.astype(jnp.int32)
+    following = jnp.where(bucket == bucket_count - 1, 0, bucket + 1)
+    same = lane == bucket
+    query_ref[rows, head_dim:] = jnp.where(same, 1.0, 0.0).astype(query_ref.dtype)
+    key_ref[rows, head_dim:] = jnp.where(same | (lane == following), 0.0, MASKED).astype(key_ref.dtype)
+
+
+def extend_received(block_ref, query_ref, key_ref, value_ref, rows, bucket_count):
+    tok_rows = (block_ref.shape[0] - PAD_ROWS) // 2
+    block = (block_ref[:tok_rows, :], block_ref[tok_rows : 2 * tok_rows, :])
+    bucket_row = block_ref[2 * tok_rows :, :].astype(jnp.float32)[:1]
+    extend(block, bucket_row, query_ref, key_ref, value_ref, rows, bucket_count)
+
+
+def products(queries, keys):
+    return lax.dot_general(queries, keys, (((1,), (1,)), ((), ())), preferred_element_type=jnp.float32)
+
+
+def replace_diagonal(score_ref, start, size, head_dim):
+    square = (size, size)
+    itself = lax.broadcasted_iota(jnp.int32, square, 0) == lax.broadcasted_iota(jnp.int32, square, 1)
+    replaced = SELF_SCORE * math.sqrt(head_dim)
+    for at in range(0, score_ref.shape[0], size):
+        columns = slice(start + at, start + at + size)
+        diagonal = score_ref[at : at + size, columns]
+        score_ref[at : at + size, columns] = jnp.where(itself, replaced, diagonal)
+
+
+def early_kernel(bucket_hbm, qk_hbm, value_hbm, *refs, bucket_count):
+    refs, (bucket_ref, own_qk_ref, own_value_ref, sems) = refs[:-4], refs[-4:]
+    block_refs, (query_ref, key_ref, value_ref, *score_refs) = refs[:-5], refs[-5:]
+    tok_rows, head_dim = own_qk_ref.shape
+    query_rows = score_refs[0].shape[0]
+    own = lax.axis_index("seq")
+    copies = block_copies(qk_hbm, value_hbm, own, own_qk_ref, own_value_ref, sems)
+    copies.append(pltpu.make_async_copy(bucket_hbm, bucket_ref, sems.at[2]))
+    for copy in copies:
+        copy.start()
+    for at, block_ref in enumerate(block_refs):
+        rows = slice((at + 1) * tok_rows, (at + 2) * tok_rows)
+        extend_received(block_ref, query_ref, key_ref, value_ref, rows, bucket_count)
+    early = slice(0, (len(block_refs) + 1) * tok_rows)
+    for copy in copies:
+        copy.wait()
+    own_block = (own_qk_ref[...], own_value_ref[...])
+    own_row = bucket_ref[pl.ds(own, 1), :].astype(jnp.float32)
+    extend(own_block, own_row, query_ref, key_ref, value_ref, slice(0, tok_rows), bucket_count)
+    for block, score_ref in enumerate(score_refs):
+        start = block * query_rows
+        score_ref[:, early] = products(query_ref[start : start + query_rows, :], key_ref[early, :])
+        replace_diagonal(score_ref, start, tok_rows, head_dim)
+
+
+def attend_early(bucket_heads, shared_qk, values, blocks, bucket_count):
+    source_count, tok_rows = bucket_heads.shape
+    head_dim = shared_qk.shape[1] // source_count
+    rows = source_count * tok_rows
+    own = pltpu.VMEM((tok_rows, head_dim), shared_qk.dtype)
+    return pl.pallas_call(
+        functools.partial(early_kernel, bucket_count=bucket_count),
+        in_specs=in_hbm(3) + in_vmem(len(blocks)),
+        out_specs=in_vmem(5),
+        out_shape=[pltpu.VMEM((rows, 2 * head_dim), shared_qk.dtype)] * 3
+        + [pltpu.VMEM((2 * tok_rows, rows), jnp.float32)] * 2,
+        scratch_shapes=[
+            pltpu.VMEM(bucket_heads.shape, bucket_heads.dtype),
+            *(own, own),
+            pltpu.SemaphoreType.DMA((3,)),
+        ],
+        compiler_params=vmem_params(8),
+        name="attend_early",
+    )(*(stays_in_hbm(array) for array in (bucket_heads, shared_qk, values)), *blocks)
+
+
+def attend_kernel(*refs, bucket_count):
+    refs, (late_score_ref, first_term_ref, second_term_ref) = refs[:-3], refs[-3:]
+    query_rows, token_count = first_term_ref.shape
+    tok_rows = query_rows // 2
+    source_count = token_count // tok_rows
     pair_count = source_count // 2
-    block_refs, refs = refs[: source_count - 1], refs[source_count - 1 :]
-    out_refs, refs = refs[:pair_count], refs[pair_count:]
-    w_ref, query_ref, key_ref, value_ref = refs[:4]
-    score_refs, term_refs = refs[4:7], refs[7:9]
-    bucket_ref, sems = refs[9:]
-    _, tok_rows, head_dim = out_refs[0].shape
-    token_count = source_count * tok_rows
+    refs, (query_ref, key_ref, value_ref, *score_refs) = refs[:-5], refs[-5:]
+    score_refs.append(late_score_ref)
+    block_refs, out_refs = refs[5:-pair_count], refs[-pair_count:]
+    head_dim = out_refs[0].shape[2]
     own = lax.axis_index("seq")
-    owners = [(-step % pair_count, (own + flip) % 2) for step, flip in (*moves(source_count), (0, 0))]
-    last = slice(token_count - tok_rows, token_count)
-    own_copies = block_copies(qk_hbm, value_hbm, own, key_ref.at[last, :head_dim], value_ref.at[last, :head_dim], sems)
-    own_copies.append(pltpu.make_async_copy(bucket_hbm, bucket_ref, sems.at[2]))
-    for copy in own_copies:
-        copy.start()
-    width = w_ref.shape[1]
-    theirs = pl.multiple_of((1 - lax.axis_index("mp")) * width, width)
-    fetch = pltpu.make_async_copy(w_hbm.at[:, pl.ds(theirs, width)], w_ref, sems.at[3])
-    fetch.start()
-    lane = lax.broadcasted_iota(jnp.int32, (tok_rows, head_dim), 1)
-
-    def prepare(source):
-        at = slice(source * tok_rows, (source + 1) * tok_rows)
-        if source < source_count - 1:
-            block_ref = block_refs[source]
-            query_ref[at, :head_dim] = block_ref[:tok_rows, :]
-            key_ref[at, :head_dim] = block_ref[:tok_rows, :]
-            value_ref[at, :head_dim] = block_ref[tok_rows : 2 * tok_rows, :]
-            row = block_ref[2 * tok_rows :, :].astype(jnp.float32)[:1]
-        else:
-            for copy in own_copies:
-                copy.wait()
-            query_ref[at, :head_dim] = key_ref[at, :head_dim]
-            row = bucket_ref[pl.ds(own, 1), :].astype(jnp.float32)
-        value_ref[at, head_dim:] = jnp.ones((tok_rows, head_dim), value_ref.dtype)
-        bucket = jnp.broadcast_to(row, (head_dim, tok_rows)).T.astype(jnp.int32)
-        following = jnp.where(bucket == bucket_count - 1, 0, bucket + 1)
-        same = lane == bucket
-        query_ref[at, head_dim:] = jnp.where(same, 1.0, 0.0).astype(query_ref.dtype)
-        key_ref[at, head_dim:] = jnp.where(same | (lane == following), 0.0, MASKED).astype(key_ref.dtype)
-
+    owners = [(-step % pair_count, (own + flip) % 2) for step, flip in ((0, 0), *moves(source_count))]
     scale = 1.0 / math.sqrt(head_dim)
     strip = 16
-    square = (tok_rows, tok_rows)
-    itself = lax.broadcasted_iota(jnp.int32, square, 0) == lax.broadcasted_iota(jnp.int32, square, 1)
-
-    def scores_of(block, score_ref, keys):
-        score_ref[:, keys] = lax.dot_general(
-            query_ref[block * query_rows : (block + 1) * query_rows, :],
-            key_ref[keys, :],
-            (((1,), (1,)), ((), ())),
-            preferred_element_type=jnp.float32,
-        )
-
-    def replace_diagonal(block, score_ref):
-        for at in range(0, query_rows, tok_rows):
-            columns = slice(block * query_rows + at, block * query_rows + at + tok_rows)
-            diagonal = score_ref[at : at + tok_rows, columns]
-            score_ref[at : at + tok_rows, columns] = jnp.where(itself, SELF_SCORE / scale, diagonal)
+    blocks = token_count // query_rows
+    ahead = 2
+
+    def scores_of(block, keys):
+        queries = query_ref[block * query_rows : (block + 1) * query_rows, :]
+        score_refs[block % 3][:, keys] = products(queries, key_ref[keys, :])
 
     def terms_of(score_ref, term_ref):
         for at in range(0, query_rows, strip):
@@ -315,48 +357,66 @@
             step, which = owners[(block * query_rows + at) // tok_rows]
             out_refs[step][which] = attended[at : at + tok_rows]
 
-    blocks = token_count // query_rows
-    ahead = min(2, blocks)
-    for tile in range(blocks):
-        stop = (tile + 1) * query_rows
-        for source in range(tile * query_rows // tok_rows, stop // tok_rows):
-            prepare(source)
-        for block in range(min(tile + 1, ahead)):
-            keys = slice(0 if tile == block else tile * query_rows, stop)
-            scores_of(block, score_refs[block], keys)
-    for block in range(ahead):
-        replace_diagonal(block, score_refs[block])
+    for at, block_ref in enumerate(block_refs):
+        stop = (source_count - len(block_refs) + at + 1) * tok_rows
+        extend_received(block_ref, query_ref, key_ref, value_ref, slice(stop - tok_rows, stop), bucket_count)
+        if stop % query_rows == 0:
+            for block in range(ahead):
+                scores_of(block, slice(stop - query_rows, stop))
     for block in range(blocks):
         if block + ahead < blocks:
-            scores_of(block + ahead, score_refs[(block + ahead) % 3], slice(0, token_count))
-            replace_diagonal(block + ahead, score_refs[(block + ahead) % 3])
-        terms_of(score_refs[block % 3], term_refs[block % 2])
-        attend_of(block, term_refs[block % 2])
-    fetch.wait()
-
-
-def attend_head(bucket_heads, shared_qk, values, w_out, blocks, bucket_count):
-    source_count, tok_rows = bucket_heads.shape
-    head_dim = shared_qk.shape[1] // source_count
-    token_count = source_count * tok_rows
-    query_rows = 2 * tok_rows
-    extended = pltpu.VMEM((token_count, 2 * head_dim), shared_qk.dtype)
-    scores = pltpu.VMEM((query_rows, token_count), jnp.float32)
-    terms = pltpu.VMEM((query_rows, token_count), shared_qk.dtype)
-    return pl.pallas_call(
-        functools.partial(attend_kernel, bucket_count=bucket_count, query_rows=query_rows),
-        in_specs=in_hbm(4) + in_vmem(len(blocks)),
-        out_specs=in_vmem(source_count // 2 + 1),
-        out_shape=[pltpu.VMEM((2, tok_rows, head_dim), shared_qk.dtype)] * (source_count // 2)
-        + [pltpu.VMEM((w_out.shape[0], w_out.shape[1] // 2), w_out.dtype)],
-        scratch_shapes=[
-            *(extended, extended, extended, scores, scores, scores, terms, terms),
-            pltpu.VMEM(bucket_heads.shape, bucket_heads.dtype),
-            pltpu.SemaphoreType.DMA((4,)),
-        ],
+            scores_of(block + ahead, slice(0, token_count))
+            replace_diagonal(score_refs[(block + ahead) % 3], (block + ahead) * query_rows, tok_rows, head_dim)
+        term_ref = (first_term_ref, second_term_ref)[block % 2]
+        terms_of(score_refs[block % 3], term_ref)
+        attend_of(block, term_ref)
+
+
+def attend_head(early, blocks, bucket_count):
+    token_count, head_dim = early[0].shape[0], early[0].shape[1] // 2
+    tok_rows = early[-1].shape[0] // 2
+    pair_count = token_count // (2 * tok_rows)
+    dtype = early[0].dtype
+    terms = pltpu.VMEM((2 * tok_rows, token_count), dtype)
+    outs = pl.pallas_call(
+        functools.partial(attend_kernel, bucket_count=bucket_count),
+        in_specs=in_vmem(len(early) + len(blocks)),
+        out_specs=in_vmem(pair_count + len(early)),
+        out_shape=[pltpu.VMEM((2, tok_rows, head_dim), dtype)] * pair_count
+        + [pltpu.VMEM(array.shape, array.dtype) for array in early],
+        input_output_aliases={at: pair_count + at for at in range(len(early))},
+        scratch_shapes=[pltpu.VMEM(early[-1].shape, early[-1].dtype), terms, terms],
         compiler_params=vmem_params(20),
         name="attend_head",
-    )(*(stays_in_hbm(array) for array in (bucket_heads, shared_qk, values, w_out)), *blocks)
+    )(*early, *blocks)
+    return outs[:pair_count]
+
+
+def fetch_kernel(w_hbm, after_ref, w_ref, sems):
+    width = w_ref.shape[1]
+    theirs = pl.multiple_of((1 - lax.axis_index("mp")) * width, width)
+    rows = w_ref.shape[0] // FETCHES
+    pieces = [slice(at * rows, (at + 1) * rows) for at in range(FETCHES)]
+    fetches = [
+        pltpu.make_async_copy(w_hbm.at[piece, pl.ds(theirs, width)], w_ref.at[piece, :], sems.at[at])
+        for at, piece in enumerate(pieces)
+    ]
+    for fetch in fetches:
+        fetch.start()
+    for fetch in fetches:
+        fetch.wait()
+
+
+def fetch_theirs(w_out, after):
+    return pl.pallas_call(
+        fetch_kernel,
+        in_specs=in_hbm(1) + in_vmem(1),
+        out_specs=in_vmem(1)[0],
+        out_shape=pltpu.VMEM((w_out.shape[0], w_out.shape[1] // 2), w_out.dtype),
+        scratch_shapes=[pltpu.SemaphoreType.DMA((FETCHES,))],
+        compiler_params=vmem_params(8),
+        name="fetch_theirs",
+    )(stays_in_hbm(w_out), after)
 
 
 def gather_kernel(*refs):
@@ -377,13 +437,15 @@
     )(*pairs)
 
 
-def widen_kernel(*refs):
-    pair_refs, (swapped_ref, w_ref, out_ref, wide_ref) = refs[:-4], refs[-4:]
-    pair_count, _, head_dim = swapped_ref.shape
+def widen_kernel(*refs, pair_count):
+    refs, (w_ref, out_ref, wide_ref) = refs[:-3], refs[-3:]
+    pair_refs, swapped_refs = refs[:pair_count], refs[pair_count:]
+    _, _, head_dim = pair_refs[0].shape
+    swapped = [ref.at[at] for ref in swapped_refs for at in range(ref.shape[0])]
     own = lax.axis_index("seq")
     for step, pair_ref in enumerate(pair_refs):
         pair = (own // 2 + pair_count - step) % pair_count
-        for rows, which in ((pair_ref[own % 2], own % 2), (swapped_ref[step], 1 - own % 2)):
+        for rows, which in ((pair_ref[own % 2], own % 2), (swapped[step][...], 1 - own % 2)):
             start = pl.multiple_of((pair * 2 + which) * head_dim, head_dim)
             wide_ref[:, pl.ds(start, head_dim)] = rows
     out_ref[...] = jnp.dot(
@@ -394,16 +456,16 @@
 def widen_and_project(pairs, swapped, w_theirs, columns):
     tok_rows = pairs[0].shape[1]
     return pl.pallas_call(
-        widen_kernel,
-        in_specs=in_vmem(len(pairs) + 2),
+        functools.partial(widen_kernel, pair_count=len(pairs)),
+        in_specs=in_vmem(len(pairs) + len(swapped) + 1),
         out_specs=in_vmem(2),
         out_shape=[
-            pltpu.VMEM((tok_rows, columns), swapped.dtype),
-            pltpu.VMEM((tok_rows, w_theirs.shape[0]), swapped.dtype),
+            pltpu.VMEM((tok_rows, columns), w_theirs.dtype),
+            pltpu.VMEM((tok_rows, w_theirs.shape[0]), w_theirs.dtype),
         ],
         compiler_params=vmem_params(16),
         name="widen_and_project",
-    )(*pairs, swapped, w_theirs)
+    )(*pairs, *swapped, w_theirs)
 
 
 def theirs_kernel(wide_ref, w_ref, out_ref, *, start):
@@ -483,9 +545,16 @@
         sent(block, step, flip)
         for (step, flip), block in zip(moves(seq_count), pack_blocks(bucket_heads, shared_qk, values))
     ]
-    *pairs, w_theirs = attend_head(bucket_heads, shared_qk, values, w_out, received, counts.shape[2])
-    pairs = pairs[:1] + [sent(pair, step, 0) for step, pair in enumerate(pairs) if step]
-    swapped = sent(gather_other(pairs), 0, 1)
+    bucket_count = counts.shape[2]
+    first_count = 2 * (5 * seq_count // 16) - 1
+    early = attend_early(bucket_heads, shared_qk, values, received[:first_count], bucket_count)
+    pairs = list(attend_head(early, received[first_count:], bucket_count))
+    w_theirs = fetch_theirs(w_out, pairs[0])
+    *others, last = pairs[1:]
+    pairs = pairs[:1] + [sent(pair, step + 1, 0) for step, pair in enumerate(others)]
+    pairs.append(sent(last, len(pairs), 0))
+    cut = len(pairs) // 2 + 1
+    swapped = [sent(gather_other(some), 0, 1) for some in (pairs[:cut], pairs[cut:])]
     columns = w_theirs.shape[1] // 4
     first, wide = widen_and_project(pairs, swapped, w_theirs, columns)
     peers = [(0, 1), (1, 0)]
@@ -499,7 +568,7 @@
 def local(shared_qk, values, buckets, counts, w_out):
     head_count = buckets.shape[1]
     seq_count = lax.axis_size("seq")
-    one_head_each = head_count == seq_count and counts.shape[2] == seq_count and 2 < seq_count <= 128 and seq_count % 2 == 0
+    one_head_each = head_count == seq_count and counts.shape[2] == seq_count and 8 <= seq_count <= 128 and seq_count % 2 == 0
     if one_head_each and lax.axis_size("mp") == 2 and 2 * shared_qk.shape[0] <= BLOCK:
         return local_by_head(shared_qk, values, buckets, counts, w_out)
     return local_by_bucket(shared_qk, values, buckets, counts, w_out)

time: 72.2 us -> 73.3 us (1.015)
  Pallas kernels: 14.3 us -> 18.1 us
  waiting for transfers between devices: 23 us -> 20.2 us
    pallas_call x1 -> x3, Pallas kernels: 0.59 us -> 5.65 us  [the longest x1 3.48 us: fetch_theirs(): pl.pallas_call(fetch_kernel, in_specs=in_hbm(1) + in_vmem(1), out_specs=i...]
    ppermute x23 -> x24, waiting for transfers between devices: 15.1 us -> 11.9 us  [sent(): lax.ppermute(block, 'seq', [(i, moved(i, step, flip, count)) for i in ran...]
    pallas_call x1, Pallas kernels: 6.37 us -> 5.15 us  [attend_head(): pl.pallas_call(functools.partial(attend_kernel, bucket_count=bucket_count...]
    ppermute x23 -> x24, starting transfers between devices: 32.4 us -> 32.5 us  [sent(): lax.ppermute(block, 'seq', [(i, moved(i, step, flip, count)) for i in ran...]
  transfers between devices with their start and end apart: 25 -> 26, of which waited for: 10 -> 9; matrix products, arithmetic and copies ran while one was open for 0% -> 0% of each run, Pallas kernels for 6% -> 12%
where the time goes in v1:
time: 73.3 us; the launch traced here: 73 us
  starting transfers between devices  34.6 us (47%)
  waiting for transfers between devices  20.2 us (28%)
  Pallas kernels  18.1 us (25%)
    ppermute x24, starting transfers between devices, sent(): lax.ppermute(block, 'seq', [(i, moved(i, step, flip, count)) for i in ran...  32.5 us
    ppermute x24, waiting for transfers between devices, sent(): lax.ppermute(block, 'seq', [(i, moved(i, step, flip, count)) for i in ran...  11.9 us
    ppermute x1, waiting for transfers between devices, local_by_head(): arrived = [lax.ppermute(first, 'mp', peers)]  8.28 us
    pallas_call x1, Pallas kernels, attend_head(): pl.pallas_call(functools.partial(attend_kernel, bucket_count=bucket_count...  5.15 us
    pallas_call x1, Pallas kernels, project_ours(): pl.pallas_call(ours_kernel, in_specs=in_vmem(1) + in_hbm(1), out_specs=in...  4 us
    pallas_call x1, Pallas kernels, fetch_theirs(): pl.pallas_call(fetch_kernel, in_specs=in_hbm(1) + in_vmem(1), out_specs=i...  3.48 us
    pallas_call x1, Pallas kernels, attend_early(): pl.pallas_call(functools.partial(early_kernel, bucket_count=bucket_count)...  1.58 us
    ppermute x1, starting transfers between devices, local_by_head(): arrived.append(lax.ppermute(rest, 'mp', peers))  1.55 us
  transfers between devices with their start and end apart: 26, of which 9 were waited for; matrix products, arithmetic and copies ran while one was open for 0% of the time, Pallas kernels for 12%

profile of v1, /device:TPU:0, one launch (start us, length us, event | category | flops | bytes accessed | tf_op | source)
XLA Modules:
  0.0 73.0 jit_solution(14221500533371508398)
XLA Ops:
  0.0 1.4 %pack_blocks.1 = (bf16[264,128]{1,0:T(8,128)(2,1)S(1)}, bf16[264,128]{1,0:T(8,128)(2,1)S(1)}, bf16[264,128]{1,0:T(8,128)(2,1)S(1)}, bf16[264,128]{1,0:T(8,128)(2...) custom-call(s32[16,128]{1,0:T(8,128)} %bitcast.1, ...), custom_call_target="tpu_custom_call" | custom-call | tf_op jit(solution)/shard_map/pack_blocks/pallas_call | solution.py:228
  1.4 3.1 %collective-permute-start = (bf16[264,128]{1,0:T(8,128)(2,1)S(1)}, bf16[264,128]{1,0:T(8,128)(2,1)S(1)}, u32[]{:S(2)}, u32[]{:S(2)}) collective-permute-start(bf16[264,128]{1,0:T(8,128)(2,1)S(1)} %get-tuple-element.35), channel_id=1, source_target_pairs={{0,8},{2,10},{4,12},{6,14},{8,16},{10,18},{12,20},{14,22},{16,24},... | collective-permute-start | bytes 202760 | tf_op jit(solution)/shard_map/ppermute | solution.py:190
  4.6 2.6 %collective-permute-start.1 = (bf16[264,128]{1,0:T(8,128)(2,1)S(1)}, bf16[264,128]{1,0:T(8,128)(2,1)S(1)}, u32[]{:S(2)}, u32[]{:S(2)}) collective-permute-start(bf16[264,128]{1,0:T(8,128)(2,1)S(1)} %get-tuple-element.36), channel_id=1, source_target_pairs={{0,16},{2,18},{4,20},{6,22},{8,24},{10,26},{12,28},{14,30},{16,0},... | collective-permute-start | bytes 202760 | tf_op jit(solution)/shard_map/ppermute | solution.py:190
  7.1 1.3 %collective-permute-start.2 = (bf16[264,128]{1,0:T(8,128)(2,1)S(1)}, bf16[264,128]{1,0:T(8,128)(2,1)S(1)}, u32[]{:S(2)}, u32[]{:S(2)}) collective-permute-start(bf16[264,128]{1,0:T(8,128)(2,1)S(1)} %get-tuple-element.37), channel_id=1, source_target_pairs={{0,24},{2,26},{4,28},{6,30},{8,0},{10,2},{12,4},{14,6},{16,8},{18,... | collective-permute-start | bytes 202760 | tf_op jit(solution)/shard_map/ppermute | solution.py:190
  9.3 2.4 %collective-permute-done.1.refs_1_ = bf16[264,128]{1,0:T(8,128)(2,1)S(1)} collective-permute-done((bf16[264,128]{1,0:T(8,128)(2,1)S(1)}, bf16[264,128]{1,0:T(8,128)(2,1)S(1)}, u32[]{:S(2)}, u32[]{:S(2)}) %collective-permute-start.1) | collective-permute-done | bytes 67616 | tf_op jit(solution)/shard_map/ppermute | solution.py:190
  12.1 1.5 %collective-permute-start.7 = (bf16[264,128]{1,0:T(8,128)(2,1)S(1)}, bf16[264,128]{1,0:T(8,128)(2,1)S(1)}, u32[]{:S(2)}, u32[]{:S(2)}) collective-permute-start(bf16[264,128]{1,0:T(8,128)(2,1)S(1)} %get-tuple-element.42), channel_id=1, source_target_pairs={{0,4},{2,6},{4,8},{6,10},{8,12},{10,14},{12,16},{14,18},{16,20},{1... | collective-permute-start | bytes 202760 | tf_op jit(solution)/shard_map/ppermute | solution.py:190
  13.6 2.0 %collective-permute-start.8 = (bf16[264,128]{1,0:T(8,128)(2,1)S(1)}, bf16[264,128]{1,0:T(8,128)(2,1)S(1)}, u32[]{:S(2)}, u32[]{:S(2)}) collective-permute-start(bf16[264,128]{1,0:T(8,128)(2,1)S(1)} %get-tuple-element.43), channel_id=1, source_target_pairs={{0,12},{2,14},{4,16},{6,18},{8,20},{10,22},{12,24},{14,26},{16,28}... | collective-permute-start | bytes 202760 | tf_op jit(solution)/shard_map/ppermute | solution.py:190
  15.7 1.8 %collective-permute-start.9 = (bf16[264,128]{1,0:T(8,128)(2,1)S(1)}, bf16[264,128]{1,0:T(8,128)(2,1)S(1)}, u32[]{:S(2)}, u32[]{:S(2)}) collective-permute-start(bf16[264,128]{1,0:T(8,128)(2,1)S(1)} %get-tuple-element.49), channel_id=1, source_target_pairs={{0,20},{2,22},{4,24},{6,26},{8,28},{10,30},{12,0},{14,2},{16,4},{1... | collective-permute-start | bytes 202760 | tf_op jit(solution)/shard_map/ppermute | solution.py:190
  17.5 3.3 %collective-permute-start.10 = (bf16[264,128]{1,0:T(8,128)(2,1)S(1)}, bf16[264,128]{1,0:T(8,128)(2,1)S(1)}, u32[]{:S(2)}, u32[]{:S(2)}) collective-permute-start(bf16[264,128]{1,0:T(8,128)(2,1)S(1)} %get-tuple-element.50), channel_id=1, source_target_pairs={{0,28},{2,30},{4,0},{6,2},{8,4},{10,6},{12,8},{14,10},{16,12},{18,... | collective-permute-start | bytes 202760 | tf_op jit(solution)/shard_map/ppermute | solution.py:190
  20.8 1.0 %collective-permute-start.11 = (bf16[264,128]{1,0:T(8,128)(2,1)S(1)}, bf16[264,128]{1,0:T(8,128)(2,1)S(1)}, u32[]{:S(2)}, u32[]{:S(2)}) collective-permute-start(bf16[264,128]{1,0:T(8,128)(2,1)S(1)} %get-tuple-element.51), channel_id=1, source_target_pairs={{0,6},{2,4},{4,10},{6,8},{8,14},{10,12},{12,18},{14,16},{16,22},{1... | collective-permute-start | bytes 202760 | tf_op jit(solution)/shard_map/ppermute | solution.py:190
  22.2 2.2 %collective-permute-done.8.refs_8_ = bf16[264,128]{1,0:T(8,128)(2,1)S(1)} collective-permute-done((bf16[264,128]{1,0:T(8,128)(2,1)S(1)}, bf16[264,128]{1,0:T(8,128)(2,1)S(1)}, u32[]{:S(2)}, u32[]{:S(2)}) %collective-permute-start.8) | collective-permute-done | bytes 67616 | tf_op jit(solution)/shard_map/ppermute | solution.py:190
  24.4 0.9 %collective-permute-start.13 = (bf16[264,128]{1,0:T(8,128)(2,1)S(1)}, bf16[264,128]{1,0:T(8,128)(2,1)S(1)}, u32[]{:S(2)}, u32[]{:S(2)}) collective-permute-start(bf16[264,128]{1,0:T(8,128)(2,1)S(1)} %get-tuple-element.53), channel_id=1, source_target_pairs={{0,22},{2,20},{4,26},{6,24},{8,30},{10,28},{12,2},{14,0},{16,6},{1... | collective-permute-start | bytes 202760 | tf_op jit(solution)/shard_map/ppermute | solution.py:190
  25.3 2.6 %collective-permute-start.14 = (bf16[264,128]{1,0:T(8,128)(2,1)S(1)}, bf16[264,128]{1,0:T(8,128)(2,1)S(1)}, u32[]{:S(2)}, u32[]{:S(2)}) collective-permute-start(bf16[264,128]{1,0:T(8,128)(2,1)S(1)} %get-tuple-element.54), channel_id=1, source_target_pairs={{0,30},{2,28},{4,2},{6,0},{8,6},{10,4},{12,10},{14,8},{16,14},{18,... | collective-permute-start | bytes 202760 | tf_op jit(solution)/shard_map/ppermute | solution.py:190
  27.9 1.6 %attend_early.1 = (bf16[2048,256]{1,0:T(8,128)(2,1)S(1)}, bf16[2048,256]{1,0:T(8,128)(2,1)S(1)}, bf16[2048,256]{1,0:T(8,128)(2,1)S(1)}, f32[256,2048]{1,0:T(8,128)S(1)}, f32[256,2048]{1,0:T(8,128)S(1)}) custom-call(s32[16,128]{1,0:T(8,128)} %bitcast.2, bf16[128,2048]{1,0:T(8,128)(2,1)} %qk_hbm.3, bf16[128,2048]{1,0:T(8,128)(2,1)} %value_hbm.3, ...), custom_call_target="tpu_custom_call" | custom-call | tf_op jit(solution)/shard_map/attend_early/pallas_call | solution.py:309
  29.5 1.2 %collective-permute-done.12.refs_8_ = bf16[264,128]{1,0:T(8,128)(2,1)S(1)} collective-permute-done((bf16[264,128]{1,0:T(8,128)(2,1)S(1)}, bf16[264,128]{1,0:T(8,128)(2,1)S(1)}, u32[]{:S(2)}, u32[]{:S(2)}) %collective-permute-start.12) | collective-permute-done | bytes 67616 | tf_op jit(solution)/shard_map/ppermute | solution.py:190
  30.8 0.8 %collective-permute-done.13.refs_9_ = bf16[264,128]{1,0:T(8,128)(2,1)S(1)} collective-permute-done((bf16[264,128]{1,0:T(8,128)(2,1)S(1)}, bf16[264,128]{1,0:T(8,128)(2,1)S(1)}, u32[]{:S(2)}, u32[]{:S(2)}) %collective-permute-start.13) | collective-permute-done | bytes 67616 | tf_op jit(solution)/shard_map/ppermute | solution.py:190
  31.6 1.4 %collective-permute-done.14.refs_10_ = bf16[264,128]{1,0:T(8,128)(2,1)S(1)} collective-permute-done((bf16[264,128]{1,0:T(8,128)(2,1)S(1)}, bf16[264,128]{1,0:T(8,128)(2,1)S(1)}, u32[]{:S(2)}, u32[]{:S(2)}) %collective-permute-start.14) | collective-permute-done | bytes 67616 | tf_op jit(solution)/shard_map/ppermute | solution.py:190
  33.0 5.2 %attend_head.1 = (bf16[2,128,128]{2,1,0:T(8,128)(2,1)S(1)}, bf16[2,128,128]{2,1,0:T(8,128)(2,1)S(1)}, bf16[2,128,128]{2,1,0:T(8,128)(2,1)S(1)}, bf16[2,128,128]{...) custom-call(bf16[2048,256]{1,0:T(8,128)(2,1)S(1)} %get-tuple-element, ...), custom_call_target="tpu_custom_call", output_to_operand_aliasing={{8}: (0, {}), {9}: (1, {}), {10}: (2, {}), {11}: (3, {}), {... | custom-call | tf_op jit(solution)/shard_map/attend_head/pallas_call | solution.py:381
  38.1 1.1 %collective-permute-start.15 = (bf16[2,128,128]{2,1,0:T(8,128)(2,1)S(1)}, bf16[2,128,128]{2,1,0:T(8,128)(2,1)S(1)}, u32[]{:S(2)}, u32[]{:S(2)}) collective-permute-start(bf16[2,128,128]{2,1,0:T(8,128)(2,1)S(1)} %get-tuple-element.56), channel_id=1, source_target_pairs={{0,4},{2,6},{4,8},{6,10},{8,12},{10,14},{12,16},{14,18},{16,20},{1... | collective-permute-start | bytes 196616 | tf_op jit(solution)/shard_map/ppermute | solution.py:190
  39.7 2.4 %collective-permute-start.17 = (bf16[2,128,128]{2,1,0:T(8,128)(2,1)S(1)}, bf16[2,128,128]{2,1,0:T(8,128)(2,1)S(1)}, u32[]{:S(2)}, u32[]{:S(2)}) collective-permute-start(bf16[2,128,128]{2,1,0:T(8,128)(2,1)S(1)} %get-tuple-element.58), channel_id=1, source_target_pairs={{0,12},{2,14},{4,16},{6,18},{8,20},{10,22},{12,24},{14,26},{16,28}... | collective-permute-start | bytes 196616 | tf_op jit(solution)/shard_map/ppermute | solution.py:190
  42.1 1.5 %collective-permute-start.18 = (bf16[2,128,128]{2,1,0:T(8,128)(2,1)S(1)}, bf16[2,128,128]{2,1,0:T(8,128)(2,1)S(1)}, u32[]{:S(2)}, u32[]{:S(2)}) collective-permute-start(bf16[2,128,128]{2,1,0:T(8,128)(2,1)S(1)} %get-tuple-element.59), channel_id=1, source_target_pairs={{0,16},{2,18},{4,20},{6,22},{8,24},{10,26},{12,28},{14,30},{16,0},... | collective-permute-start | bytes 196616 | tf_op jit(solution)/shard_map/ppermute | solution.py:190
  43.6 2.4 %collective-permute-start.19 = (bf16[2,128,128]{2,1,0:T(8,128)(2,1)S(1)}, bf16[2,128,128]{2,1,0:T(8,128)(2,1)S(1)}, u32[]{:S(2)}, u32[]{:S(2)}) collective-permute-start(bf16[2,128,128]{2,1,0:T(8,128)(2,1)S(1)} %get-tuple-element.60), channel_id=1, source_target_pairs={{0,20},{2,22},{4,24},{6,26},{8,28},{10,30},{12,0},{14,2},{16,4},{1... | collective-permute-start | bytes 196616 | tf_op jit(solution)/shard_map/ppermute | solution.py:190
  46.0 0.8 %collective-permute-start.20 = (bf16[2,128,128]{2,1,0:T(8,128)(2,1)S(1)}, bf16[2,128,128]{2,1,0:T(8,128)(2,1)S(1)}, u32[]{:S(2)}, u32[]{:S(2)}) collective-permute-start(bf16[2,128,128]{2,1,0:T(8,128)(2,1)S(1)} %get-tuple-element.61), channel_id=1, source_target_pairs={{0,24},{2,26},{4,28},{6,30},{8,0},{10,2},{12,4},{14,6},{16,8},{18,... | collective-permute-start | bytes 196616 | tf_op jit(solution)/shard_map/ppermute | solution.py:190
  46.9 1.8 %collective-permute-start.21 = (bf16[2,128,128]{2,1,0:T(8,128)(2,1)S(1)}, bf16[2,128,128]{2,1,0:T(8,128)(2,1)S(1)}, u32[]{:S(2)}, u32[]{:S(2)}) collective-permute-start(bf16[2,128,128]{2,1,0:T(8,128)(2,1)S(1)} %get-tuple-element.62), channel_id=1, source_target_pairs={{0,28},{2,30},{4,0},{6,2},{8,4},{10,6},{12,8},{14,10},{16,12},{18,... | collective-permute-start | bytes 196616 | tf_op jit(solution)/shard_map/ppermute | solution.py:190
  48.7 2.1 %collective-permute-done.17.refs_3_ = bf16[2,128,128]{2,1,0:T(8,128)(2,1)S(1)} collective-permute-done((bf16[2,128,128]{2,1,0:T(8,128)(2,1)S(1)}, bf16[2,128,128]{2,1,0:T(8,128)(2,1)S(1)}, u32[]{:S(2)}, u32[]{:S(2)}) %collective-permute-start.17) | collective-permute-done | bytes 65568 | tf_op jit(solution)/shard_map/ppermute | solution.py:190
  51.1 1.5 %collective-permute-done.20.refs_1_.refs_6_ = bf16[2,128,128]{2,1,0:T(8,128)(2,1)S(1)} collective-permute-done((bf16[2,128,128]{2,1,0:T(8,128)(2,1)S(1)}, bf16[2,128,128]{2,1,0:T(8,128)(2,1)S(1)}, u32[]{:S(2)}, u32[]{:S(2)}) %collective-permute-start.20) | collective-permute-done | bytes 65568 | tf_op jit(solution)/shard_map/ppermute | solution.py:190
  52.7 3.5 %fetch_theirs.1.refs_10_.w_ref = bf16[2048,2048]{1,0:T(8,128)(2,1)S(1)} custom-call(bf16[2048,4096]{1,0:T(8,128)(2,1)} %w_hbm.3, bf16[2,128,128]{2,1,0:T(8,128)(2,1)S(1)} %get-tuple-element.55.refs_0_.after_ref), custom_call_target="tpu_custom_call" | custom-call | tf_op jit(solution)/shard_map/fetch_theirs/pallas_call | solution.py:411
  56.8 1.0 %project_theirs.1 = bf16[128,1536]{1,0:T(8,128)(2,1)S(1)} custom-call(bf16[128,2048]{1,0:T(8,128)(2,1)S(1)} %get-tuple-element.63.wide_ref, bf16[2048,2048]{1,0:T(8,128)(2,1)S(1)} %fetch_theirs.1.refs_10_.w_ref), custom_call_target="tpu_custom_call" | custom-call | tf_op jit(solution)/shard_map/project_theirs/pallas_call | solution.py:478
  57.8 1.5 %collective-permute-start.25 = (bf16[128,1536]{1,0:T(8,128)(2,1)S(1)}, bf16[128,1536]{1,0:T(8,128)(2,1)S(1)}, u32[]{:S(2)}, u32[]{:S(2)}) collective-permute-start(bf16[128,1536]{1,0:T(8,128)(2,1)S(1)} %project_theirs.1), channel_id=1, source_target_pairs={{0,1},{1,0},{2,3},{3,2},{4,5},{5,4},{6,7},{7,6},{8,9},{9,8},{10,11... | collective-permute-start | bytes 1179656 | tf_op jit(solution)/shard_map/ppermute | solution.py:563
  59.9 4.0 %project_ours.1.ours_ref = f32[128,2048]{1,0:T(8,128)S(1)} custom-call(bf16[128,2048]{1,0:T(8,128)(2,1)S(1)} %get-tuple-element.63.wide_ref, bf16[2048,4096]{1,0:T(8,128)(2,1)} %w_hbm.3), custom_call_target="tpu_custom_call" | custom-call | tf_op jit(solution)/shard_map/project_ours/pallas_call | solution.py:508
  63.9 8.3 %collective-permute-done.24.refs_0_ = bf16[128,512]{1,0:T(8,128)(2,1)S(1)} collective-permute-done((bf16[128,512]{1,0:T(8,128)(2,1)S(1)}, bf16[128,512]{1,0:T(8,128)(2,1)S(1)}, u32[]{:S(2)}, u32[]{:S(2)}) %collective-permute-start.24) | collective-permute-done | bytes 131104 | tf_op jit(solution)/shard_map/ppermute | solution.py:561
  72.2 0.9 %add_parts.1 = bf16[128,2048]{1,0:T(8,128)(2,1)} custom-call(f32[128,2048]{1,0:T(8,128)S(1)} %project_ours.1.ours_ref, bf16[128,512]{1,0:T(8,128)(2,1)S(1)} %collective-permute-done.24.refs_0_, bf16[128,1536]{1,0:T(8,128)(2,1)S(1)} %collective-permute-done.25.refs_1_), custom_call_target="tpu_custom_call" | custom-call | tf_op jit(solution)/shard_map/add_parts/pallas_call | solution.py:532
  (30 shorter events, 3.7 us)
Async XLA Ops:
  1.4 7.8 %collective-permute-start = (bf16[264,128]{1,0:T(8,128)(2,1)S(1)}, bf16[264,128]{1,0:T(8,128)(2,1)S(1)}, u32[]{:S(2)}, u32[]{:S(2)}) collective-permute-start(bf16[264,128]{1,0:T(8,128)(2,1)S(1)} %get-tuple-element.35), channel_id=1, source_target_pairs={{0,8},{2,10},{4,12},{6,14},{8,16},{10,18},{12,20},{14,22},{16,24},... | collective-permute-start | bytes 202760 | tf_op jit(solution)/shard_map/ppermute | solution.py:190
  4.6 7.2 %collective-permute-start.1 = (bf16[264,128]{1,0:T(8,128)(2,1)S(1)}, bf16[264,128]{1,0:T(8,128)(2,1)S(1)}, u32[]{:S(2)}, u32[]{:S(2)}) collective-permute-start(bf16[264,128]{1,0:T(8,128)(2,1)S(1)} %get-tuple-element.36), channel_id=1, source_target_pairs={{0,16},{2,18},{4,20},{6,22},{8,24},{10,26},{12,28},{14,30},{16,0},... | collective-permute-start | bytes 202760 | tf_op jit(solution)/shard_map/ppermute | solution.py:190
  7.1 5.0 %collective-permute-start.2 = (bf16[264,128]{1,0:T(8,128)(2,1)S(1)}, bf16[264,128]{1,0:T(8,128)(2,1)S(1)}, u32[]{:S(2)}, u32[]{:S(2)}) collective-permute-start(bf16[264,128]{1,0:T(8,128)(2,1)S(1)} %get-tuple-element.37), channel_id=1, source_target_pairs={{0,24},{2,26},{4,28},{6,30},{8,0},{10,2},{12,4},{14,6},{16,8},{18,... | collective-permute-start | bytes 202760 | tf_op jit(solution)/shard_map/ppermute | solution.py:190
  8.5 5.1 %collective-permute-start.3 = (bf16[264,128]{1,0:T(8,128)(2,1)S(1)}, bf16[264,128]{1,0:T(8,128)(2,1)S(1)}, u32[]{:S(2)}, u32[]{:S(2)}) collective-permute-start(bf16[264,128]{1,0:T(8,128)(2,1)S(1)} %get-tuple-element.38), channel_id=1, source_target_pairs={{0,2},{2,0},{4,6},{6,4},{8,10},{10,8},{12,14},{14,12},{16,18},{18,... | collective-permute-start | bytes 202760 | tf_op jit(solution)/shard_map/ppermute | solution.py:190
  8.5 7.2 %collective-permute-start.4 = (bf16[264,128]{1,0:T(8,128)(2,1)S(1)}, bf16[264,128]{1,0:T(8,128)(2,1)S(1)}, u32[]{:S(2)}, u32[]{:S(2)}) collective-permute-start(bf16[264,128]{1,0:T(8,128)(2,1)S(1)} %get-tuple-element.39), channel_id=1, source_target_pairs={{0,10},{2,8},{4,14},{6,12},{8,18},{10,16},{12,22},{14,20},{16,26},... | collective-permute-start | bytes 202760 | tf_op jit(solution)/shard_map/ppermute | solution.py:190
  9.3 8.2 %collective-permute-start.5 = (bf16[264,128]{1,0:T(8,128)(2,1)S(1)}, bf16[264,128]{1,0:T(8,128)(2,1)S(1)}, u32[]{:S(2)}, u32[]{:S(2)}) collective-permute-start(bf16[264,128]{1,0:T(8,128)(2,1)S(1)} %get-tuple-element.40), channel_id=1, source_target_pairs={{0,18},{2,16},{4,22},{6,20},{8,26},{10,24},{12,30},{14,28},{16,2},... | collective-permute-start | bytes 202760 | tf_op jit(solution)/shard_map/ppermute | solution.py:190
  11.7 9.0 %collective-permute-start.6 = (bf16[264,128]{1,0:T(8,128)(2,1)S(1)}, bf16[264,128]{1,0:T(8,128)(2,1)S(1)}, u32[]{:S(2)}, u32[]{:S(2)}) collective-permute-start(bf16[264,128]{1,0:T(8,128)(2,1)S(1)} %get-tuple-element.41), channel_id=1, source_target_pairs={{0,26},{2,24},{4,30},{6,28},{8,2},{10,0},{12,6},{14,4},{16,10},{18... | collective-permute-start | bytes 202760 | tf_op jit(solution)/shard_map/ppermute | solution.py:190
  12.1 9.7 %collective-permute-start.7 = (bf16[264,128]{1,0:T(8,128)(2,1)S(1)}, bf16[264,128]{1,0:T(8,128)(2,1)S(1)}, u32[]{:S(2)}, u32[]{:S(2)}) collective-permute-start(bf16[264,128]{1,0:T(8,128)(2,1)S(1)} %get-tuple-element.42), channel_id=1, source_target_pairs={{0,4},{2,6},{4,8},{6,10},{8,12},{10,14},{12,16},{14,18},{16,20},{1... | collective-permute-start | bytes 202760 | tf_op jit(solution)/shard_map/ppermute | solution.py:190
  13.6 10.7 %collective-permute-start.8 = (bf16[264,128]{1,0:T(8,128)(2,1)S(1)}, bf16[264,128]{1,0:T(8,128)(2,1)S(1)}, u32[]{:S(2)}, u32[]{:S(2)}) collective-permute-start(bf16[264,128]{1,0:T(8,128)(2,1)S(1)} %get-tuple-element.43), channel_id=1, source_target_pairs={{0,12},{2,14},{4,16},{6,18},{8,20},{10,22},{12,24},{14,26},{16,28}... | collective-permute-start | bytes 202760 | tf_op jit(solution)/shard_map/ppermute | solution.py:190
  15.7 9.7 %collective-permute-start.9 = (bf16[264,128]{1,0:T(8,128)(2,1)S(1)}, bf16[264,128]{1,0:T(8,128)(2,1)S(1)}, u32[]{:S(2)}, u32[]{:S(2)}) collective-permute-start(bf16[264,128]{1,0:T(8,128)(2,1)S(1)} %get-tuple-element.49), channel_id=1, source_target_pairs={{0,20},{2,22},{4,24},{6,26},{8,28},{10,30},{12,0},{14,2},{16,4},{1... | collective-permute-start | bytes 202760 | tf_op jit(solution)/shard_map/ppermute | solution.py:190
  17.5 12.1 %collective-permute-start.10 = (bf16[264,128]{1,0:T(8,128)(2,1)S(1)}, bf16[264,128]{1,0:T(8,128)(2,1)S(1)}, u32[]{:S(2)}, u32[]{:S(2)}) collective-permute-start(bf16[264,128]{1,0:T(8,128)(2,1)S(1)} %get-tuple-element.50), channel_id=1, source_target_pairs={{0,28},{2,30},{4,0},{6,2},{8,4},{10,6},{12,8},{14,10},{16,12},{18,... | collective-permute-start | bytes 202760 | tf_op jit(solution)/shard_map/ppermute | solution.py:190
  20.8 8.8 %collective-permute-start.11 = (bf16[264,128]{1,0:T(8,128)(2,1)S(1)}, bf16[264,128]{1,0:T(8,128)(2,1)S(1)}, u32[]{:S(2)}, u32[]{:S(2)}) collective-permute-start(bf16[264,128]{1,0:T(8,128)(2,1)S(1)} %get-tuple-element.51), channel_id=1, source_target_pairs={{0,6},{2,4},{4,10},{6,8},{8,14},{10,12},{12,18},{14,16},{16,22},{1... | collective-permute-start | bytes 202760 | tf_op jit(solution)/shard_map/ppermute | solution.py:190
  21.8 9.0 %collective-permute-start.12 = (bf16[264,128]{1,0:T(8,128)(2,1)S(1)}, bf16[264,128]{1,0:T(8,128)(2,1)S(1)}, u32[]{:S(2)}, u32[]{:S(2)}) collective-permute-start(bf16[264,128]{1,0:T(8,128)(2,1)S(1)} %get-tuple-element.52), channel_id=1, source_target_pairs={{0,14},{2,12},{4,18},{6,16},{8,22},{10,20},{12,26},{14,24},{16,30}... | collective-permute-start | bytes 202760 | tf_op jit(solution)/shard_map/ppermute | solution.py:190
  24.4 7.2 %collective-permute-start.13 = (bf16[264,128]{1,0:T(8,128)(2,1)S(1)}, bf16[264,128]{1,0:T(8,128)(2,1)S(1)}, u32[]{:S(2)}, u32[]{:S(2)}) collective-permute-start(bf16[264,128]{1,0:T(8,128)(2,1)S(1)} %get-tuple-element.53), channel_id=1, source_target_pairs={{0,22},{2,20},{4,26},{6,24},{8,30},{10,28},{12,2},{14,0},{16,6},{1... | collective-permute-start | bytes 202760 | tf_op jit(solution)/shard_map/ppermute | solution.py:190
  25.3 7.6 %collective-permute-start.14 = (bf16[264,128]{1,0:T(8,128)(2,1)S(1)}, bf16[264,128]{1,0:T(8,128)(2,1)S(1)}, u32[]{:S(2)}, u32[]{:S(2)}) collective-permute-start(bf16[264,128]{1,0:T(8,128)(2,1)S(1)} %get-tuple-element.54), channel_id=1, source_target_pairs={{0,30},{2,28},{4,2},{6,0},{8,6},{10,4},{12,10},{14,8},{16,14},{18,... | collective-permute-start | bytes 202760 | tf_op jit(solution)/shard_map/ppermute | solution.py:190
  38.1 7.9 %collective-permute-start.15 = (bf16[2,128,128]{2,1,0:T(8,128)(2,1)S(1)}, bf16[2,128,128]{2,1,0:T(8,128)(2,1)S(1)}, u32[]{:S(2)}, u32[]{:S(2)}) collective-permute-start(bf16[2,128,128]{2,1,0:T(8,128)(2,1)S(1)} %get-tuple-element.56), channel_id=1, source_target_pairs={{0,4},{2,6},{4,8},{6,10},{8,12},{10,14},{12,16},{14,18},{16,20},{1... | collective-permute-start | bytes 196616 | tf_op jit(solution)/shard_map/ppermute | solution.py:190
  39.2 7.7 %collective-permute-start.16 = (bf16[2,128,128]{2,1,0:T(8,128)(2,1)S(1)}, bf16[2,128,128]{2,1,0:T(8,128)(2,1)S(1)}, u32[]{:S(2)}, u32[]{:S(2)}) collective-permute-start(bf16[2,128,128]{2,1,0:T(8,128)(2,1)S(1)} %get-tuple-element.57), channel_id=1, source_target_pairs={{0,8},{2,10},{4,12},{6,14},{8,16},{10,18},{12,20},{14,22},{16,24},... | collective-permute-start | bytes 196616 | tf_op jit(solution)/shard_map/ppermute | solution.py:190
  39.7 11.0 %collective-permute-start.17 = (bf16[2,128,128]{2,1,0:T(8,128)(2,1)S(1)}, bf16[2,128,128]{2,1,0:T(8,128)(2,1)S(1)}, u32[]{:S(2)}, u32[]{:S(2)}) collective-permute-start(bf16[2,128,128]{2,1,0:T(8,128)(2,1)S(1)} %get-tuple-element.58), channel_id=1, source_target_pairs={{0,12},{2,14},{4,16},{6,18},{8,20},{10,22},{12,24},{14,26},{16,28}... | collective-permute-start | bytes 196616 | tf_op jit(solution)/shard_map/ppermute | solution.py:190
  42.1 8.9 %collective-permute-start.18 = (bf16[2,128,128]{2,1,0:T(8,128)(2,1)S(1)}, bf16[2,128,128]{2,1,0:T(8,128)(2,1)S(1)}, u32[]{:S(2)}, u32[]{:S(2)}) collective-permute-start(bf16[2,128,128]{2,1,0:T(8,128)(2,1)S(1)} %get-tuple-element.59), channel_id=1, source_target_pairs={{0,16},{2,18},{4,20},{6,22},{8,24},{10,26},{12,28},{14,30},{16,0},... | collective-permute-start | bytes 196616 | tf_op jit(solution)/shard_map/ppermute | solution.py:190
  43.6 7.5 %collective-permute-start.19 = (bf16[2,128,128]{2,1,0:T(8,128)(2,1)S(1)}, bf16[2,128,128]{2,1,0:T(8,128)(2,1)S(1)}, u32[]{:S(2)}, u32[]{:S(2)}) collective-permute-start(bf16[2,128,128]{2,1,0:T(8,128)(2,1)S(1)} %get-tuple-element.60), channel_id=1, source_target_pairs={{0,20},{2,22},{4,24},{6,26},{8,28},{10,30},{12,0},{14,2},{16,4},{1... | collective-permute-start | bytes 196616 | tf_op jit(solution)/shard_map/ppermute | solution.py:190
  46.0 6.6 %collective-permute-start.20 = (bf16[2,128,128]{2,1,0:T(8,128)(2,1)S(1)}, bf16[2,128,128]{2,1,0:T(8,128)(2,1)S(1)}, u32[]{:S(2)}, u32[]{:S(2)}) collective-permute-start(bf16[2,128,128]{2,1,0:T(8,128)(2,1)S(1)} %get-tuple-element.61), channel_id=1, source_target_pairs={{0,24},{2,26},{4,28},{6,30},{8,0},{10,2},{12,4},{14,6},{16,8},{18,... | collective-permute-start | bytes 196616 | tf_op jit(solution)/shard_map/ppermute | solution.py:190
  46.9 5.7 %collective-permute-start.21 = (bf16[2,128,128]{2,1,0:T(8,128)(2,1)S(1)}, bf16[2,128,128]{2,1,0:T(8,128)(2,1)S(1)}, u32[]{:S(2)}, u32[]{:S(2)}) collective-permute-start(bf16[2,128,128]{2,1,0:T(8,128)(2,1)S(1)} %get-tuple-element.62), channel_id=1, source_target_pairs={{0,28},{2,30},{4,0},{6,2},{8,4},{10,6},{12,8},{14,10},{16,12},{18,... | collective-permute-start | bytes 196616 | tf_op jit(solution)/shard_map/ppermute | solution.py:190
  51.0 5.1 %collective-permute-start.22 = (bf16[5,128,128]{2,1,0:T(8,128)(2,1)S(1)}, bf16[5,128,128]{2,1,0:T(8,128)(2,1)S(1)}, u32[]{:S(2)}, u32[]{:S(2)}) collective-permute-start(bf16[5,128,128]{2,1,0:T(8,128)(2,1)S(1)} %gather_other.2), channel_id=1, source_target_pairs={{0,2},{2,0},{4,6},{6,4},{8,10},{10,8},{12,14},{14,12},{16,18},{18,... | collective-permute-start | bytes 491528 | tf_op jit(solution)/shard_map/ppermute | solution.py:190
  52.6 3.6 %collective-permute-start.23 = (bf16[3,128,128]{2,1,0:T(8,128)(2,1)S(1)}, bf16[3,128,128]{2,1,0:T(8,128)(2,1)S(1)}, u32[]{:S(2)}, u32[]{:S(2)}) collective-permute-start(bf16[3,128,128]{2,1,0:T(8,128)(2,1)S(1)} %gather_other.3), channel_id=1, source_target_pairs={{0,2},{2,0},{4,6},{6,4},{8,10},{10,8},{12,14},{14,12},{16,18},{18,... | collective-permute-start | bytes 294920 | tf_op jit(solution)/shard_map/ppermute | solution.py:190
  57.8 14.4 %collective-permute-start.25 = (bf16[128,1536]{1,0:T(8,128)(2,1)S(1)}, bf16[128,1536]{1,0:T(8,128)(2,1)S(1)}, u32[]{:S(2)}, u32[]{:S(2)}) collective-permute-start(bf16[128,1536]{1,0:T(8,128)(2,1)S(1)} %project_theirs.1), channel_id=1, source_target_pairs={{0,1},{1,0},{2,3},{3,2},{4,5},{5,4},{6,7},{7,6},{8,9},{9,8},{10,11... | collective-permute-start | bytes 1179656 | tf_op jit(solution)/shard_map/ppermute | solution.py:563
  59.3 12.8 %collective-permute-start.24 = (bf16[128,512]{1,0:T(8,128)(2,1)S(1)}, bf16[128,512]{1,0:T(8,128)(2,1)S(1)}, u32[]{:S(2)}, u32[]{:S(2)}) collective-permute-start(bf16[128,512]{1,0:T(8,128)(2,1)S(1)} %get-tuple-element.64), channel_id=1, source_target_pairs={{0,1},{1,0},{2,3},{3,2},{4,5},{5,4},{6,7},{7,6},{8,9},{9,8},{10,11... | collective-permute-start | bytes 393224 | tf_op jit(solution)/shard_map/ppermute | solution.py:561
